TPU v7x, 1024 devices: a whole 4x4x32 slice. The times are simulated.
1024 devices in a mesh: row: 32 (over x, z_hi, core), col: 32 (over z_lo, y).
Axes of the slice: x: 4, y: 4, z: 32 (z_hi: 4, z_lo: 8; z = z_hi * 8 + z_lo), core: 2. Of those that a mesh axis runs over, the one named last changes fastest.
Arguments:
- stem: bfloat16 [2, 512, 131072], P(None, None, ('row', 'col')), may hold values from -6 to 6
- left_pool: bfloat16 [32, 2, 512, 512], P('row'), may hold values from -0.1875 to 0.1875
- right_pool: bfloat16 [32, 2, 2, 512, 512], P('row'), may hold values from -0.1875 to 0.1875
- owners: int32 [3], replicated, may hold values from 0 to 31, as said below
- slices: int32 [3], replicated, may hold values from 0 to 1, as said below
- relabels: int32 [2, 512], replicated, may hold values from 0 to 511, each once within a row
Outputs:
- amplitudes: bfloat16 [2, 512, 131072], P(None, None, ('row', 'col'))
Inputs may be any that keep to these rules, and one draw needn't show every extreme that they name: `owners`: the 3 entries are distinct pool entries. `slices`: the 3 entries are not all equal.
All inputs are finite; a program needn't handle non-finite values.
Results may differ from a plain program's by a relative error of at most 0.0075.
Values may be sent and summed in bfloat16 or wider, within the bound.
No kernel may reach another device: no remote copies, remote signals or barrier semaphores. Data moves between devices by JAX's collectives and lax.ppermute only.
A program may use at most 32 MiB of HBM per device.

v0:
```python
import jax
import jax.numpy as jnp
from jax import lax
from jax.sharding import PartitionSpec as P

CONTRACTIONS = 3


def broadcast(block, axis, owner):
    block = jnp.where(lax.axis_index(axis) == owner, block, jnp.zeros_like(block))
    return lax.psum(block, axis)


def complex_product(first, second):
    real = jnp.dot(first[0], second[0], preferred_element_type=jnp.float32) - jnp.dot(
        first[1], second[1], preferred_element_type=jnp.float32
    )
    imaginary = jnp.dot(first[0], second[1], preferred_element_type=jnp.float32) + jnp.dot(
        first[1], second[0], preferred_element_type=jnp.float32
    )
    return jnp.stack([real, imaginary]).astype(jnp.bfloat16)


def fetch_branch(left_pool, right_pool, root, chosen):
    left_local = left_pool[0]
    right_local = lax.dynamic_index_in_dim(right_pool[0], chosen, 0, keepdims=False)
    holder = lax.axis_index("row") == root
    local_branch = lax.cond(
        holder,
        lambda: complex_product(left_local, right_local),
        lambda: jnp.zeros(left_local.shape, jnp.bfloat16),
    )
    return broadcast(local_branch, "row", root)


def regroup_apply(blocks, worker):
    return worker(lax.all_to_all(blocks, "col", split_axis=1, concat_axis=1, tiled=True))


def body(stem, left_pool, right_pool, owners, slices, relabels):
    branches = []
    for section in range(CONTRACTIONS):
        branches.append(fetch_branch(left_pool, right_pool, owners[section], slices[section]))
    state = complex_product(branches[0], stem)
    groups = lax.axis_size("col")
    width = state.shape[1]
    for section in range(1, CONTRACTIONS):
        mapping = relabels[section - 1]
        blocks = state.reshape(2, groups, width // groups, state.shape[2])
        moved = jnp.take(branches[section], jnp.argsort(mapping, stable=True), axis=2)

        def worker(piece, moved=moved):
            return complex_product(moved, piece.reshape(2, width, piece.shape[3]))

        state = regroup_apply(blocks, worker)
    return state


def solution(mesh):
    in_specs = (
        P(None, None, ("row", "col")),
        P("row", None, None, None),
        P("row", None, None, None, None),
        P(),
        P(),
        P(),
    )
    out_specs = P(None, None, ("row", "col"))
    return jax.shard_map(body, mesh=mesh, in_specs=in_specs, out_specs=out_specs, check_vma=False)
```

profile of v0, /device:TPU:8, one launch (start us, length us, event | category | flops | bytes accessed | tf_op | source)
XLA Modules:
  0.0 660.4 jit_solution(525079395094184768)
XLA Ops:
  6.5 0.0 all-reduce.3.cloned.1.call-start
  6.5 1.4 fusion.96
  9.9 1.6 conditional.3
  9.9 1.5 broadcast.11.clone
  11.4 1.8 broadcast_select_fusion.4
  13.2 1.5 conditional.4
  13.2 1.5 broadcast.12.clone
  14.8 1.5 conditional.5
  14.8 1.5 broadcast.13.clone
  16.3 3.1 broadcast_select_fusion.2
  19.3 0.0 all-reduce.3.cloned.1.call-update
  19.4 568.8 %all-reduce.3.cloned.1.call-done = (bf16[2,512,512]{1,0,2:T(2,128)(2,1)}, bf16[2,512,512]{1,0,2:T(2,128)(2,1)}, bf16[2,512,512]{1,0,2:T(2,128)(2,1)}) async-done(((bf16[2,512,512]{1,0,2:T(2,128)(2,1)}, bf16[2,512,512]{1,0,2:T(2,128)(2,1)}, bf16[2,512,512]{1,0,2:T(2,128)(2,1)}), (bf16[2,512,512]{1,0,2:T(2,128)(2,1)}, bf16[2,512,512]{1,0,2:T(2,128)(2,1)}, ...) | async-done | bytes 3145744 | tf_op jit(solution)/shard_map/psum | solution.py:11
  588.2 0.0 copy-start.8
  588.2 3.4 fusion.92
  591.6 1.3 copy.24
  592.9 0.0 copy-done.8
  592.9 0.3 fusion.72
  593.2 0.3 fusion.70
  593.5 0.0 copy-start.9
  593.5 0.0 copy-start.7
  593.6 1.3 copy.25
  594.9 0.3 fusion.54
  595.2 0.3 fusion.55
  595.5 0.7 pad_maximum_fusion.3
  596.2 10.8 %all-to-all-start = ((bf16[2,32,16,128]{3,2,0,1:T(8,128)(2,1)}), bf16[2,32,16,128]{3,2,0,1:T(8,128)(2,1)S(1)}, u32[]{:S(2)}, u32[]{:S(2)}) async-start(bf16[2,32,16,128]{3,2,0,1:T(8,128)(2,1)} %pad_maximum_fusion.3), calls=%async_computation | async-start | bytes 524288 | tf_op jit(solution)/shard_map/all_to_all | solution.py:37
  607.0 0.0 copy-done.9
  607.0 3.8 sort.32
  610.8 0.0 copy-done.7
  610.8 3.6 gather_fusion.1
  614.4 2.0 fusion.63
  616.3 1.5 fusion.91
  617.8 1.3 copy.22
  619.2 1.3 copy.28
  620.5 3.6 all-to-all-done
  624.1 0.3 fusion.76
  624.4 0.0 copy-start.6
  624.4 0.3 fusion.74
  624.8 0.3 fusion.56
  625.1 0.3 fusion.57
  625.4 0.7 pad_maximum_fusion.4
  626.1 9.0 %all-to-all-start.1 = ((bf16[2,32,16,128]{3,2,0,1:T(8,128)(2,1)}), bf16[2,32,16,128]{3,2,0,1:T(8,128)(2,1)S(1)}, u32[]{:S(2)}, u32[]{:S(2)}) async-start(bf16[2,32,16,128]{3,2,0,1:T(8,128)(2,1)} %pad_maximum_fusion.4), calls=%async_computation.1 | async-start | bytes 524288 | tf_op jit(solution)/shard_map/all_to_all | solution.py:37
  635.1 3.8 sort.31
  638.9 0.0 copy-done.6
  638.9 3.6 gather_fusion
  642.4 2.0 fusion.62
  644.4 1.5 fusion.90
  645.9 1.3 copy.20
  647.2 1.3 copy.31
  648.6 3.1 all-to-all-done.1
  651.7 0.3 fusion.80
  651.9 0.3 fusion.78
  652.2 0.3 fusion.61
  652.6 0.3 fusion.60
  652.9 0.7 pad_maximum_fusion.5
  (11 shorter events, 0.1 us)
Async XLA Ops:
  6.5 581.7 %all-reduce.3.cloned.1.call-start = ((), (), s32[]{:S(2)}) async-start(), calls=%async_computation.2 | async-start | bytes 6291456 | tf_op jit(solution)/shard_map/psum | solution.py:11
  588.2 4.7 copy-start.8
  593.5 13.4 %copy-start.9 = (s32[2,512]{1,0:T(2,128)S(1)}, s32[2,512]{1,0:T(2,128)}, u32[]{:S(2)}) copy-start(s32[2,512]{1,0:T(2,128)} %param.19) | copy-start | bytes 12292
  593.5 17.2 %copy-start.7 = (bf16[2,512,512]{1,0,2:T(2,128)(2,1)S(1)}, bf16[2,512,512]{1,0,2:T(2,128)(2,1)}, u32[]{:S(2)}) copy-start(bf16[2,512,512]{1,0,2:T(2,128)(2,1)} %get-tuple-element.161) | copy-start | bytes 3145732
  596.2 27.9 %all-to-all-start = ((bf16[2,32,16,128]{3,2,0,1:T(8,128)(2,1)}), bf16[2,32,16,128]{3,2,0,1:T(8,128)(2,1)S(1)}, u32[]{:S(2)}, u32[]{:S(2)}) async-start(bf16[2,32,16,128]{3,2,0,1:T(8,128)(2,1)} %pad_maximum_fusion.3), calls=%async_computation | async-start | bytes 524288 | tf_op jit(solution)/shard_map/all_to_all | solution.py:37
  624.4 14.4 %copy-start.6 = (bf16[2,512,512]{1,0,2:T(2,128)(2,1)S(1)}, bf16[2,512,512]{1,0,2:T(2,128)(2,1)}, u32[]{:S(2)}) copy-start(bf16[2,512,512]{1,0,2:T(2,128)(2,1)} %get-tuple-element.162) | copy-start | bytes 3145732
  626.1 25.5 %all-to-all-start.1 = ((bf16[2,32,16,128]{3,2,0,1:T(8,128)(2,1)}), bf16[2,32,16,128]{3,2,0,1:T(8,128)(2,1)S(1)}, u32[]{:S(2)}, u32[]{:S(2)}) async-start(bf16[2,32,16,128]{3,2,0,1:T(8,128)(2,1)} %pad_maximum_fusion.4), calls=%async_computation.1 | async-start | bytes 524288 | tf_op jit(solution)/shard_map/all_to_all | solution.py:37
Sparse Core Ops, SparseCore 0:
  19.5 568.6 all-reduce.2
where the time goes:
time: 661 us; the launch traced here: 660 us
  waiting for transfers between devices  576 us (87%)
  local copies, waits for them, and re-layouts  27.5 us (4%)
  starting transfers between devices  19.7 us (3%)
  other arithmetic  18.6 us (3%)
  between operations  15.6 us (2%)
    psum x1, waiting for transfers between devices, broadcast(): return lax.psum(block, axis)  569 us
    all_to_all x2, starting transfers between devices, regroup_apply(): lax.all_to_all(blocks, 'col', split_axis=1, concat_axis=1, tiled=True)  19.7 us
  transfers between devices with their start and end apart: 3, of which 3 were waited for; matrix products, arithmetic and copies ran while one was open for 4% of the time, Pallas kernels for 0%

commit v1 on v0

v1 whole, which is shorter than its diff:
```python
import functools

import jax
import jax.numpy as jnp
from jax import lax
from jax.experimental import pallas as pl
from jax.experimental.pallas import tpu as pltpu
from jax.sharding import Mesh
from jax.sharding import PartitionSpec as P

PARTS = (("x", 4), ("zh", 4), ("core", 2), ("zl", 8), ("y", 4))
ALL = tuple(name for name, _ in PARTS)
ROW, COL = ALL[:3], ALL[3:]
SPREAD, PLANE = ("x", "core"), ("x", "y")
TILE = (16, 128)
F32, BF16 = jnp.float32, jnp.bfloat16


def own_row():
    return (lax.axis_index("x") * 4 + lax.axis_index("zh")) * 2 + lax.axis_index("core")


def slice_kernel(owners, slices, relabels, left, right, out):
    row = own_row()
    used = [owners[k] == row for k in range(3)]
    chosen = jnp.int32(0)
    for k in range(3):
        chosen = jnp.where(used[k], slices[k], chosen)
    block = lax.axis_index("y") * 8 + lax.axis_index("zl")
    rows = pl.ds(pl.multiple_of(block * 16, 16), 16)
    both = jnp.concatenate([left[0, 0, rows, :], left[0, 1, rows, :]], axis=0)
    by_real = jnp.dot(both, right[0, chosen, 0], preferred_element_type=F32)
    by_imag = jnp.dot(both, right[0, chosen, 1], preferred_element_type=F32)
    real = by_real[:16] - by_imag[16:]
    imag = by_imag[:16] + by_real[16:]
    branch = jnp.concatenate([real, imag], axis=0).astype(BF16)
    place = lax.broadcasted_iota(jnp.int32, (512, 512), 0)
    mapping = lax.broadcasted_iota(jnp.int32, (1, 512), 1)
    mapping = jnp.where(used[1], relabels[0:1, :], mapping)
    mapping = jnp.where(used[2], relabels[1:2, :], mapping)
    onehot = jnp.where(place == mapping, 1.0, 0.0).astype(BF16)
    moved = lax.dot_general(branch, onehot, (((1,), (1,)), ((), ())), preferred_element_type=F32).astype(BF16)
    for part in range(2):
        for block in range(4):
            out[block * 2 + part] = moved[part * 16 : part * 16 + 16, block * 128 : block * 128 + 128]


def branch_slice(owners, slices, relabels, left, right):
    smem, vmem = pl.BlockSpec(memory_space=pltpu.SMEM), pl.BlockSpec(memory_space=pltpu.VMEM)
    return pl.pallas_call(
        slice_kernel,
        in_specs=[smem, smem, vmem, vmem, vmem],
        out_specs=vmem,
        out_shape=jax.ShapeDtypeStruct((8, *TILE), BF16),
        name="branch_slice",
    )(owners, slices, relabels, left, right)


def contract_kernel(own, other, state, out, *, pick):
    parts = []
    for ref in (own, other):
        value = ref[...] if pick is None else ref[:, :, pick]
        columns = [value[c * 4 : c * 4 + 4].reshape(512, 128) for c in range(4)]
        parts.append(jnp.concatenate(columns, axis=1))
    if len(state.shape) == 4:
        real, imag = state[:, 0].reshape(512, 128), state[:, 1].reshape(512, 128)
    else:
        real, imag = state[0], state[1]
    both = jnp.concatenate([real, imag], axis=1)
    by_own = jnp.dot(parts[0], both, preferred_element_type=F32)
    by_other = jnp.dot(parts[1], both, preferred_element_type=F32)
    swapped = lax.axis_index("core") == 1
    by_real = jnp.where(swapped, by_other, by_own)
    by_imag = jnp.where(swapped, by_own, by_other)
    real = (by_real[:, :128] - by_imag[:, 128:]).astype(BF16)
    imag = (by_real[:, 128:] + by_imag[:, :128]).astype(BF16)
    if len(out.shape) == 4:
        out[:, 0] = real.reshape(32, *TILE)
        out[:, 1] = imag.reshape(32, *TILE)
    else:
        out[0] = real
        out[1] = imag


def contract(own, other, state, shape, pick=None):
    vmem = pl.BlockSpec(memory_space=pltpu.VMEM)
    return pl.pallas_call(
        functools.partial(contract_kernel, pick=pick),
        in_specs=[vmem, vmem, vmem],
        out_specs=vmem,
        out_shape=jax.ShapeDtypeStruct(shape, BF16),
        compiler_params=pltpu.CompilerParams(vmem_limit_bytes=16 << 20),
        name="contract",
    )(own, other, state)


def send(blocks, axes):
    return lax.all_to_all(blocks, axes, 0, 0, tiled=True)


def to_all(block, axes, count):
    return send(jnp.broadcast_to(block[None], (count, *block.shape)), axes)


def body(stem, left, right, owners, slices, relabels):
    at_x, at_zh, at_core = owners // 8, (owners // 2) % 4, owners % 2
    tiles = send(branch_slice(owners, slices, relabels, left, right), SPREAD)
    mine = [lax.dynamic_index_in_dim(tiles, at_x[k] * 2 + at_core[k], 0, keepdims=False) for k in range(3)]
    shares = to_all(jnp.stack(mine), "zh", 4)
    shares = jnp.stack([lax.dynamic_index_in_dim(shares, at_zh[k], 0, keepdims=False)[k] for k in range(3)])
    shares = to_all(shares, "zl", 8)
    held = to_all(shares, PLANE, 16)
    first, rest = held[:, :, 0], held[:, :, 1:]
    first_other, rest_other = (lax.ppermute(part, "core", [(0, 1), (1, 0)]) for part in (first, rest))
    state = contract(first, first_other, stem, (32, 2, *TILE))
    state = contract(rest, rest_other, send(state, COL), (32, 2, *TILE), 0)
    return contract(rest, rest_other, send(state, COL), (2, 512, 128), 1)


def solution(mesh):
    fine = Mesh(mesh.devices.reshape([size for _, size in PARTS]), ALL)
    in_specs = (
        P(None, None, ALL),
        P(ROW, None, None, None),
        P(ROW, None, None, None, None),
        P(),
        P(),
        P(),
    )
    return jax.shard_map(body, mesh=fine, in_specs=in_specs, out_specs=P(None, None, ALL), check_vma=False)
```

time: 661 us -> 164 us (0.25)
  waiting for transfers between devices: 576 us -> 34.2 us
  blocking collectives: 0 us -> 66.9 us
  local copies, waits for them, and re-layouts: 27.5 us -> 4.83 us
  starting transfers between devices: 19.7 us -> 42 us
  other arithmetic: 18.6 us -> 0.03 us
    psum x1 -> x0, waiting for transfers between devices: 569 us -> none  [broadcast(): return lax.psum(block, axis)]
    all_to_all x0 -> x3, blocking collectives: none -> 66.9 us  [send(): return lax.all_to_all(blocks, axes, 0, 0, tiled=True)]
    all_to_all x2 -> x3, waiting for transfers between devices: 6.68 us -> 29.7 us  [send(): return lax.all_to_all(blocks, axes, 0, 0, tiled=True)]
    all_to_all x2 -> x3, starting transfers between devices: 19.7 us -> 38.2 us  [send(): return lax.all_to_all(blocks, axes, 0, 0, tiled=True)]
    slice x13 -> x4, local copies, waits for them, and re-layouts: 15.7 us -> 2.71 us  [the longest x1 1.39 us: body(): first, rest = (held[:, :, 0], held[:, :, 1:])]
    select_n x6 -> x1, other arithmetic: 8.83 us -> 0.02 us  [body(): at_x, at_zh, at_core = (owners // 8, owners // 2 % 4, owners % 2)]
    sort x2 -> x0, other arithmetic: 7.53 us -> none  [body(): jnp.argsort(mapping, stable=True)]
    gather x2 -> x0, local copies, waits for them, and re-layouts: 7.11 us -> none  [body(): jnp.take(branches[section], jnp.argsort(mapping, stable=True), axis=2)]
  transfers between devices with their start and end apart: 3 -> 5, of which waited for: 3 -> 5; matrix products, arithmetic and copies ran while one was open for 4% -> 2% of each run, Pallas kernels for 0% -> 0%
where the time goes in v1:
time: 164 us; the launch traced here: 163 us
  blocking collectives  66.9 us (41%)
  starting transfers between devices  42 us (26%)
  waiting for transfers between devices  34.2 us (21%)
  between operations  9.32 us (6%)
  Pallas kernels  5.79 us (4%)
  local copies, waits for them, and re-layouts  4.83 us (3%)
    all_to_all x3, blocking collectives, send(): return lax.all_to_all(blocks, axes, 0, 0, tiled=True)  66.9 us
    all_to_all x3, starting transfers between devices, send(): return lax.all_to_all(blocks, axes, 0, 0, tiled=True)  38.2 us
    all_to_all x3, waiting for transfers between devices, send(): return lax.all_to_all(blocks, axes, 0, 0, tiled=True)  29.7 us
    ppermute x2, waiting for transfers between devices, body(): lax.ppermute(part, 'core', [(0, 1), (1, 0)])  4.5 us
    ppermute x2, starting transfers between devices, body(): lax.ppermute(part, 'core', [(0, 1), (1, 0)])  3.83 us
  transfers between devices with their start and end apart: 5, of which 5 were waited for; matrix products, arithmetic and copies ran while one was open for 2% of the time, Pallas kernels for 0%

profile of v1, /device:TPU:8, one launch (start us, length us, event | category | flops | bytes accessed | tf_op | source)
XLA Modules:
  0.0 163.2 jit_solution(5460014234283499338)
XLA Ops:
  0.0 0.0 copy-start.2
  0.0 3.1 %branch_slice.1 = bf16[8,16,128]{2,1,0:T(8,128)(2,1)} custom-call(s32[3]{0:T(128)} %owners.1, s32[3]{0:T(128)} %slices.1, s32[2,512]{1,0:T(2,128)} %relabels.1, bf16[1,2,512,512]{3,2,1,0:T(8,128)(2,1)} %left.1, bf16[1,2,2,512,512]{4,3,2,1,0:T(8,128)(2,1)} %right.1), custom_call_target="tpu_custom_call" | custom-call | tf_op jit(solution)/shard_map/branch_slice/pallas_call | solution.py:50
  3.1 4.3 %all-to-all-start = ((bf16[8,16,128]{2,1,0:T(8,128)(2,1)}), bf16[8,16,128]{2,1,0:T(8,128)(2,1)S(1)}, u32[]{:S(2)}, u32[]{:S(2)}) async-start(bf16[8,16,128]{2,1,0:T(8,128)(2,1)} %branch_slice.1), calls=%async_computation | async-start | bytes 65536 | tf_op jit(solution)/shard_map/all_to_all | solution.py:98
  7.4 0.0 copy-done.2
  7.4 0.7 fusion.1
  8.1 0.6 fusion.3
  12.6 0.3 all-to-all-done
  12.8 0.6 broadcast_in_dim.6
  13.5 28.3 %all-to-all-start.1 = ((bf16[4,3,16,128]{3,2,1,0:T(8,128)(2,1)}), bf16[4,3,16,128]{3,2,1,0:T(8,128)(2,1)S(1)}, u32[]{:S(2)}, u32[]{:S(2)}) async-start(bf16[4,3,16,128]{3,2,1,0:T(8,128)(2,1)} %broadcast_in_dim.6), calls=%async_computation.1 | async-start | bytes 98304 | tf_op jit(solution)/shard_map/all_to_all | solution.py:98
  47.2 17.1 %all-to-all-done.1 = bf16[4,3,16,128]{3,2,1,0:T(8,128)(2,1)S(1)} async-done(((bf16[4,3,16,128]{3,2,1,0:T(8,128)(2,1)}), bf16[4,3,16,128]{3,2,1,0:T(8,128)(2,1)S(1)}, u32[]{:S(2)}, u32[]{:S(2)}) %all-to-all-start.1) | async-done | bytes 49184 | tf_op jit(solution)/shard_map/all_to_all | solution.py:98
  64.3 16.2 %all_to_all.30 = bf16[8,3,16,128]{3,2,1,0:T(8,128)(2,1)S(1)} all-to-all(bf16[8,3,16,128]{3,2,1,0:T(8,128)(2,1)S(1)} %broadcast_in_dim.7), channel_id=1, replica_groups=mesh['x'=4,'zh'=4,'core'=2,'zl'=8,'y'=4] {'zl'}, dimensions={0} | all-to-all | bytes 196608 | tf_op jit(solution)/shard_map/all_to_all | solution.py:98
  80.6 0.3 broadcast_in_dim.8
  80.9 0.0 copy-start
  80.9 26.5 %all_to_all.31 = bf16[16,8,3,16,128]{4,3,2,1,0:T(8,128)(2,1)S(1)} all-to-all(bf16[16,8,3,16,128]{4,3,2,1,0:T(8,128)(2,1)S(1)} %broadcast_in_dim.8), channel_id=1, replica_groups=mesh['x'=4,'zh'=4,'core'=2,'zl'=8,'y'=4] {'x','y'}, dimensions={0} | all-to-all | bytes 3145728 | tf_op jit(solution)/shard_map/all_to_all | solution.py:98
  107.4 0.0 copy-start.1
  107.4 1.1 copy-done.1
  108.5 1.9 %collective-permute-start.1 = (bf16[16,8,16,128]{3,2,1,0:T(8,128)(2,1)S(1)}, bf16[16,8,16,128]{3,2,1,0:T(8,128)(2,1)S(1)}, u32[]{:S(2)}, u32[]{:S(2)}) collective-permute-start(bf16[16,8,16,128]{3,2,1,0:T(8,128)(2,1)S(1)} %slice_bitcast_fusion.own), channel_id=1, source_target_pairs={{0,32},{32,0},{1,33},{33,1},{2,34},{34,2},{3,35},{35,3},{4,36},{36... | collective-permute-start | bytes 1572872 | tf_op jit(solution)/shard_map/ppermute | solution.py:114
  110.5 1.9 %collective-permute-done.1.other = bf16[16,8,16,128]{3,2,1,0:T(8,128)(2,1)S(1)} collective-permute-done((bf16[16,8,16,128]{3,2,1,0:T(8,128)(2,1)S(1)}, bf16[16,8,16,128]{3,2,1,0:T(8,128)(2,1)S(1)}, u32[]{:S(2)}, u32[]{:S(2)}) %collective-permute-start.1) | collective-permute-done | bytes 524320 | tf_op jit(solution)/shard_map/ppermute | solution.py:114
  112.3 0.0 copy-done
  112.3 1.1 contract.3
  113.5 5.6 %all-to-all-start.4 = ((bf16[32,2,16,128]{3,2,1,0:T(8,128)(2,1)}), bf16[32,2,16,128]{3,2,1,0:T(8,128)(2,1)S(1)}, u32[]{:S(2)}, u32[]{:S(2)}) async-start(bf16[32,2,16,128]{3,2,1,0:T(8,128)(2,1)} %contract.3), calls=%async_computation.4 | async-start | bytes 524288 | tf_op jit(solution)/shard_map/all_to_all | solution.py:98
  119.1 1.4 slice.68.own
  120.5 1.9 %collective-permute-start = (bf16[16,8,2,16,128]{4,3,2,1,0:T(8,128)(2,1)S(1)}, bf16[16,8,2,16,128]{4,3,2,1,0:T(8,128)(2,1)S(1)}, u32[]{:S(2)}, u32[]{:S(2)}) collective-permute-start(bf16[16,8,2,16,128]{4,3,2,1,0:T(8,128)(2,1)S(1)} %slice.68.own), channel_id=1, source_target_pairs={{0,32},{32,0},{1,33},{33,1},{2,34},{34,2},{3,35},{35,3},{4,36},{36... | collective-permute-start | bytes 3145736 | tf_op jit(solution)/shard_map/ppermute | solution.py:114
  122.4 2.6 %collective-permute-done.other = bf16[16,8,2,16,128]{4,3,2,1,0:T(8,128)(2,1)S(1)} collective-permute-done((bf16[16,8,2,16,128]{4,3,2,1,0:T(8,128)(2,1)S(1)}, bf16[16,8,2,16,128]{4,3,2,1,0:T(8,128)(2,1)S(1)}, u32[]{:S(2)}, u32[]{:S(2)}) %collective-permute-start) | collective-permute-done | bytes 1048608 | tf_op jit(solution)/shard_map/ppermute | solution.py:114
  125.0 12.4 %all-to-all-done.4.state = bf16[32,2,16,128]{3,2,1,0:T(8,128)(2,1)S(1)} async-done(((bf16[32,2,16,128]{3,2,1,0:T(8,128)(2,1)}), bf16[32,2,16,128]{3,2,1,0:T(8,128)(2,1)S(1)}, u32[]{:S(2)}, u32[]{:S(2)}) %all-to-all-start.4) | async-done | bytes 262176 | tf_op jit(solution)/shard_map/all_to_all | solution.py:98
  137.4 0.4 contract.4
  137.8 24.2 %all_to_all.32.state = bf16[32,2,16,128]{3,2,1,0:T(8,128)(2,1)S(1)} all-to-all(bf16[32,2,16,128]{3,2,1,0:T(8,128)(2,1)S(1)} %contract.4), channel_id=1, replica_groups=mesh['x'=4,'zh'=4,'core'=2,'zl'=8,'y'=4] {'zl','y'}, dimensions={0} | all-to-all | bytes 524288 | tf_op jit(solution)/shard_map/all_to_all | solution.py:98
  162.1 1.1 contract.5
  (7 shorter events, 0.1 us)
Async XLA Ops:
  0.0 7.4 %copy-start.2 = (s32[3]{0:T(128)S(1)}, s32[3]{0:T(128)}, u32[]{:S(2)}) copy-start(s32[3]{0:T(128)} %owners.1) | copy-start | bytes 40
  3.1 9.7 %all-to-all-start = ((bf16[8,16,128]{2,1,0:T(8,128)(2,1)}), bf16[8,16,128]{2,1,0:T(8,128)(2,1)S(1)}, u32[]{:S(2)}, u32[]{:S(2)}) async-start(bf16[8,16,128]{2,1,0:T(8,128)(2,1)} %branch_slice.1), calls=%async_computation | async-start | bytes 65536 | tf_op jit(solution)/shard_map/all_to_all | solution.py:98
  13.5 50.8 %all-to-all-start.1 = ((bf16[4,3,16,128]{3,2,1,0:T(8,128)(2,1)}), bf16[4,3,16,128]{3,2,1,0:T(8,128)(2,1)S(1)}, u32[]{:S(2)}, u32[]{:S(2)}) async-start(bf16[4,3,16,128]{3,2,1,0:T(8,128)(2,1)} %broadcast_in_dim.6), calls=%async_computation.1 | async-start | bytes 98304 | tf_op jit(solution)/shard_map/all_to_all | solution.py:98
  80.9 31.5 %copy-start = (bf16[2,512,128]{2,1,0:T(8,128)(2,1)S(1)}, bf16[2,512,128]{2,1,0:T(8,128)(2,1)}, u32[]{:S(2)}) copy-start(bf16[2,512,128]{2,1,0:T(8,128)(2,1)} %state.1) | copy-start | bytes 786436
  107.4 1.2 copy-start.1
  108.5 3.8 %collective-permute-start.1 = (bf16[16,8,16,128]{3,2,1,0:T(8,128)(2,1)S(1)}, bf16[16,8,16,128]{3,2,1,0:T(8,128)(2,1)S(1)}, u32[]{:S(2)}, u32[]{:S(2)}) collective-permute-start(bf16[16,8,16,128]{3,2,1,0:T(8,128)(2,1)S(1)} %slice_bitcast_fusion.own), channel_id=1, source_target_pairs={{0,32},{32,0},{1,33},{33,1},{2,34},{34,2},{3,35},{35,3},{4,36},{36... | collective-permute-start | bytes 1572872 | tf_op jit(solution)/shard_map/ppermute | solution.py:114
  113.5 23.9 %all-to-all-start.4 = ((bf16[32,2,16,128]{3,2,1,0:T(8,128)(2,1)}), bf16[32,2,16,128]{3,2,1,0:T(8,128)(2,1)S(1)}, u32[]{:S(2)}, u32[]{:S(2)}) async-start(bf16[32,2,16,128]{3,2,1,0:T(8,128)(2,1)} %contract.3), calls=%async_computation.4 | async-start | bytes 524288 | tf_op jit(solution)/shard_map/all_to_all | solution.py:98
  120.5 4.6 %collective-permute-start = (bf16[16,8,2,16,128]{4,3,2,1,0:T(8,128)(2,1)S(1)}, bf16[16,8,2,16,128]{4,3,2,1,0:T(8,128)(2,1)S(1)}, u32[]{:S(2)}, u32[]{:S(2)}) collective-permute-start(bf16[16,8,2,16,128]{4,3,2,1,0:T(8,128)(2,1)S(1)} %slice.68.own), channel_id=1, source_target_pairs={{0,32},{32,0},{1,33},{33,1},{2,34},{34,2},{3,35},{35,3},{4,36},{36... | collective-permute-start | bytes 3145736 | tf_op jit(solution)/shard_map/ppermute | solution.py:114

commit v2 on v1

v2 whole, which is shorter than its diff:
```python
import jax
import jax.numpy as jnp
from jax import lax
from jax.experimental import pallas as pl
from jax.experimental.pallas import tpu as pltpu
from jax.sharding import Mesh
from jax.sharding import PartitionSpec as P

PARTS = (("x", 4), ("zh", 4), ("core", 2), ("za", 2), ("zb", 4), ("y", 4))
ALL = tuple(name for name, _ in PARTS)
ROW, COL = ALL[:3], ALL[3:]
SPREAD, LINE, PLANE, NEAR = ("x", "core"), ("za", "zb"), ("x", "y"), ("core", "zb", "y")
TILE = (16, 128)
FLIP = [(0, 1), (1, 0)]
F32, BF16 = jnp.float32, jnp.bfloat16


def own_row():
    return (lax.axis_index("x") * 4 + lax.axis_index("zh")) * 2 + lax.axis_index("core")


def slice_kernel(owners, slices, relabels, left, right, out):
    row = own_row()
    used = [owners[k] == row for k in range(3)]
    chosen = jnp.int32(0)
    for k in range(3):
        chosen = jnp.where(used[k], slices[k], chosen)
    at_z, at_y = lax.axis_index("za") * 4 + lax.axis_index("zb"), lax.axis_index("y")
    block = jnp.where(used[0], at_z * 4 + at_y, at_y * 8 + at_z)
    rows = pl.ds(pl.multiple_of(block * 16, 16), 16)
    both = jnp.concatenate([left[0, 0, rows, :], left[0, 1, rows, :]], axis=0)
    by_real = jnp.dot(both, right[0, chosen, 0], preferred_element_type=F32)
    by_imag = jnp.dot(both, right[0, chosen, 1], preferred_element_type=F32)
    real = by_real[:16] - by_imag[16:]
    imag = by_imag[:16] + by_real[16:]
    branch = jnp.concatenate([real, imag], axis=0).astype(BF16)
    q = lax.broadcasted_iota(jnp.int32, (512, 512), 0)
    arrived = (((q >> 3) & 1) << 8) | (((q >> 4) & 15) << 4) | (((q >> 8) & 1) << 3) | (q & 7)
    place = jnp.where(used[1], arrived, q)
    mapping = lax.broadcasted_iota(jnp.int32, (1, 512), 1)
    mapping = jnp.where(used[1], relabels[0:1, :], mapping)
    mapping = jnp.where(used[2], relabels[1:2, :], mapping)
    onehot = jnp.where(place == mapping, 1.0, 0.0).astype(BF16)
    moved = lax.dot_general(branch, onehot, (((1,), (1,)), ((), ())), preferred_element_type=F32)
    halves = jnp.concatenate([moved[:8], moved[16:24], moved[8:16], moved[24:]], axis=0)
    moved = jnp.where(used[0], halves, moved).astype(BF16)
    for c in range(4):
        for h in range(2):
            out[c * 2 + h] = moved[h * 16 : h * 16 + 16, c * 128 : c * 128 + 128]


VMEM = pl.BlockSpec(memory_space=pltpu.VMEM)
SMEM = pl.BlockSpec(memory_space=pltpu.SMEM)
SMALL = pltpu.CompilerParams(vmem_limit_bytes=16 << 20)


def branch_slice(owners, slices, relabels, left, right):
    return pl.pallas_call(
        slice_kernel,
        in_specs=[SMEM, SMEM, VMEM, VMEM, VMEM],
        out_specs=VMEM,
        out_shape=jax.ShapeDtypeStruct((8, *TILE), BF16),
        name="branch_slice",
    )(owners, slices, relabels, left, right)


def first_kernel(held, *refs):
    *stems, out = refs
    branch = jnp.concatenate([held[c * 4 : c * 4 + 4, :4].reshape(256, 128) for c in range(4)], axis=1)
    results = []
    for stem in stems:
        both = jnp.concatenate([stem[0], stem[1]], axis=1)
        by = jnp.dot(branch, both, preferred_element_type=F32).reshape(16, 2, 8, 256)
        real = by[:, 0, :, :128] - by[:, 1, :, 128:]
        imag = by[:, 0, :, 128:] + by[:, 1, :, :128]
        results.append((real, imag))
    core, ahead = lax.axis_index("core"), lax.axis_index("za") == 1
    for flip in range(2):
        target = jnp.bitwise_xor(core, flip)
        for part in range(2):
            near, far = results[flip][part], results[2 + flip][part]
            low, high = jnp.where(ahead, far, near), jnp.where(ahead, near, far)
            tiles = jnp.concatenate([low, high], axis=1).astype(BF16)
            for y in range(4):
                for zb in range(4):
                    out[target, zb * 4 + y, part] = tiles[y * 4 + zb]


def first_contract(held, stems):
    return pl.pallas_call(
        first_kernel,
        in_specs=[VMEM] * 5,
        out_specs=VMEM,
        out_shape=jax.ShapeDtypeStruct((2, 16, 2, *TILE), BF16),
        compiler_params=SMALL,
        name="first_contract",
    )(held, *stems)


def make_contract_kernel(pick):
    def kernel(own, other, state, out):
        parts = []
        for ref in (own, other):
            columns = [ref[c * 4 : c * 4 + 4, pick].reshape(512, 128) for c in range(4)]
            parts.append(jnp.concatenate(columns, axis=1))
        both = jnp.concatenate([state[:, 0].reshape(512, 128), state[:, 1].reshape(512, 128)], axis=1)
        by_own = jnp.dot(parts[0], both, preferred_element_type=F32)
        by_other = jnp.dot(parts[1], both, preferred_element_type=F32)
        swapped = lax.axis_index("core") == 1
        by_real = jnp.where(swapped, by_other, by_own)
        by_imag = jnp.where(swapped, by_own, by_other)
        real = (by_real[:, :128] - by_imag[:, 128:]).astype(BF16)
        imag = (by_real[:, 128:] + by_imag[:, :128]).astype(BF16)
        if len(out.shape) == 4:
            out[:, 0] = real.reshape(32, *TILE)
            out[:, 1] = imag.reshape(32, *TILE)
        else:
            out[0] = real
            out[1] = imag

    return kernel


def contract(own, other, state, shape, pick):
    return pl.pallas_call(
        make_contract_kernel(pick),
        in_specs=[VMEM] * 3,
        out_specs=VMEM,
        out_shape=jax.ShapeDtypeStruct(shape, BF16),
        compiler_params=SMALL,
        name="contract",
    )(own, other, state)


def send(blocks, axes):
    return lax.all_to_all(blocks, axes, 0, 0, tiled=True)


def to_all(block, axes, count):
    return send(jnp.broadcast_to(block[None], (count, *block.shape)), axes)


def body(stem, left, right, owners, slices, relabels):
    at_x, at_zh, at_core = owners // 8, (owners // 2) % 4, owners % 2
    across = lax.ppermute(stem, "za", FLIP)
    stems = (stem, lax.ppermute(stem, "core", FLIP), across, lax.ppermute(across, "core", FLIP))
    tiles = send(branch_slice(owners, slices, relabels, left, right), SPREAD)
    mine = [lax.dynamic_index_in_dim(tiles, at_x[k] * 2 + at_core[k], 0, keepdims=False) for k in range(3)]
    shares = to_all(jnp.stack(mine), "zh", 4)
    shares = jnp.stack([lax.dynamic_index_in_dim(shares, at_zh[k], 0, keepdims=False)[k] for k in range(3)])
    shares = to_all(shares, LINE, 8)
    first = lax.dynamic_slice_in_dim(shares[:, 0], lax.axis_index("za") * 4, 4, 0)
    held = to_all(jnp.concatenate([first, shares[:, 1], shares[:, 2]]), PLANE, 16)
    state = first_contract(held, stems).reshape(32, 2, *TILE)
    own = held[:, 4:].reshape(16, 2, 8, *TILE)
    other = lax.ppermute(own, "core", FLIP)
    state = contract(own, other, send(state, NEAR), (32, 2, *TILE), 0)
    return contract(own, other, send(state, COL), (2, 512, 128), 1)


def solution(mesh):
    fine = Mesh(mesh.devices.reshape([size for _, size in PARTS]), ALL)
    in_specs = (
        P(None, None, ALL),
        P(ROW, None, None, None),
        P(ROW, None, None, None, None),
        P(),
        P(),
        P(),
    )
    return jax.shard_map(body, mesh=fine, in_specs=in_specs, out_specs=P(None, None, ALL), check_vma=False)
```

time: 164 us -> 165 us (level)
  the two profiles are of different devices: /device:TPU:8 before, /device:TPU:2 now
where the time goes in v2:
time: 165 us
  waiting for transfers between devices  61.6 us (37%)
  starting transfers between devices  59 us (36%)
  blocking collectives  24.4 us (15%)
  between operations  9.64 us (6%)
  Pallas kernels  5.83 us (4%)
  local copies, waits for them, and re-layouts  4.17 us (3%)
    all_to_all x5, starting transfers between devices, send(): return lax.all_to_all(blocks, axes, 0, 0, tiled=True)  50.6 us
    all_to_all x5, waiting for transfers between devices, send(): return lax.all_to_all(blocks, axes, 0, 0, tiled=True)  34.8 us
    all_to_all x1, blocking collectives, send(): return lax.all_to_all(blocks, axes, 0, 0, tiled=True)  24.4 us
    ppermute x1, waiting for transfers between devices, body(): across = lax.ppermute(stem, 'za', FLIP)  22.9 us
  transfers between devices with their start and end apart: 9, of which 6 were waited for; matrix products, arithmetic and copies ran while one was open for 1% of the time, Pallas kernels for 0%

profile of v2, /device:TPU:2, one launch (start us, length us, event | category | flops | bytes accessed | tf_op | source)
XLA Modules:
  0.0 164.6 jit_solution(10241663912787522459)
XLA Ops:
  0.0 0.0 copy-start.1
  0.0 3.1 %branch_slice.1 = bf16[8,16,128]{2,1,0:T(8,128)(2,1)} custom-call(s32[3]{0:T(128)} %owners.1, s32[3]{0:T(128)} %slices.1, s32[2,512]{1,0:T(2,128)} %relabels.1, bf16[1,2,512,512]{3,2,1,0:T(8,128)(2,1)} %left.1, bf16[1,2,2,512,512]{4,3,2,1,0:T(8,128)(2,1)} %right.1), custom_call_target="tpu_custom_call" | custom-call | tf_op jit(solution)/shard_map/branch_slice/pallas_call | solution.py:58
  3.1 16.4 %all-to-all-start = ((bf16[8,16,128]{2,1,0:T(8,128)(2,1)}), bf16[8,16,128]{2,1,0:T(8,128)(2,1)S(1)}, u32[]{:S(2)}, u32[]{:S(2)}) async-start(bf16[8,16,128]{2,1,0:T(8,128)(2,1)} %branch_slice.1), calls=%async_computation | async-start | bytes 65536 | tf_op jit(solution)/shard_map/all_to_all | solution.py:136
  19.5 0.0 copy-done.1
  19.5 0.7 fusion.2
  20.2 0.6 fusion.4
  24.7 0.0 all-to-all-done
  24.8 0.6 broadcast_in_dim.6
  25.4 16.8 %all-to-all-start.1 = ((bf16[4,3,16,128]{3,2,1,0:T(8,128)(2,1)}), bf16[4,3,16,128]{3,2,1,0:T(8,128)(2,1)S(1)}, u32[]{:S(2)}, u32[]{:S(2)}) async-start(bf16[4,3,16,128]{3,2,1,0:T(8,128)(2,1)} %broadcast_in_dim.6), calls=%async_computation.1 | async-start | bytes 98304 | tf_op jit(solution)/shard_map/all_to_all | solution.py:136
  47.8 16.9 %all-to-all-done.1 = bf16[4,3,16,128]{3,2,1,0:T(8,128)(2,1)S(1)} async-done(((bf16[4,3,16,128]{3,2,1,0:T(8,128)(2,1)}), bf16[4,3,16,128]{3,2,1,0:T(8,128)(2,1)S(1)}, u32[]{:S(2)}, u32[]{:S(2)}) %all-to-all-start.1) | async-done | bytes 49184 | tf_op jit(solution)/shard_map/all_to_all | solution.py:136
  64.7 0.7 broadcast_in_dim.7
  65.3 5.2 %all-to-all-start.2 = ((bf16[8,3,16,128]{3,2,1,0:T(8,128)(2,1)}), bf16[8,3,16,128]{3,2,1,0:T(8,128)(2,1)S(1)}, u32[]{:S(2)}, u32[]{:S(2)}) async-start(bf16[8,3,16,128]{3,2,1,0:T(8,128)(2,1)} %broadcast_in_dim.7), calls=%async_computation.2 | async-start | bytes 196608 | tf_op jit(solution)/shard_map/all_to_all | solution.py:136
  70.6 11.2 %all-to-all-done.2 = bf16[8,3,16,128]{3,2,1,0:T(8,128)(2,1)S(1)} async-done(((bf16[8,3,16,128]{3,2,1,0:T(8,128)(2,1)}), bf16[8,3,16,128]{3,2,1,0:T(8,128)(2,1)S(1)}, u32[]{:S(2)}, u32[]{:S(2)}) %all-to-all-start.2) | async-done | bytes 98336 | tf_op jit(solution)/shard_map/all_to_all | solution.py:136
  81.8 1.3 broadcast_in_dim.8
  83.1 0.0 copy-start
  83.1 7.6 %all-to-all-start.3 = ((bf16[16,20,16,128]{3,2,1,0:T(8,128)(2,1)}), bf16[16,20,16,128]{3,2,1,0:T(8,128)(2,1)S(1)}, u32[]{:S(2)}, u32[]{:S(2)}) async-start(bf16[16,20,16,128]{3,2,1,0:T(8,128)(2,1)} %broadcast_in_dim.8), calls=%async_computation.3 | async-start | bytes 2621440 | tf_op jit(solution)/shard_map/all_to_all | solution.py:136
  90.7 0.0 copy-done
  90.7 2.3 %collective-permute-start.2 = (bf16[2,512,128]{2,1,0:T(8,128)(2,1)S(1)}, bf16[2,512,128]{2,1,0:T(8,128)(2,1)S(1)}, u32[]{:S(2)}, u32[]{:S(2)}) collective-permute-start(bf16[2,512,128]{2,1,0:T(8,128)(2,1)S(1)} %copy-done), channel_id=1, source_target_pairs={{0,16},{16,0},{1,17},{17,1},{2,18},{18,2},{3,19},{19,3},{4,20},{20... | collective-permute-start | bytes 786440 | tf_op jit(solution)/shard_map/ppermute | solution.py:145
  93.1 1.9 %collective-permute-start.1 = (bf16[2,512,128]{2,1,0:T(8,128)(2,1)S(1)}, bf16[2,512,128]{2,1,0:T(8,128)(2,1)S(1)}, u32[]{:S(2)}, u32[]{:S(2)}) collective-permute-start(bf16[2,512,128]{2,1,0:T(8,128)(2,1)S(1)} %copy-done), channel_id=1, source_target_pairs={{0,32},{32,0},{1,33},{33,1},{2,34},{34,2},{3,35},{35,3},{4,36},{36... | collective-permute-start | bytes 786440 | tf_op jit(solution)/shard_map/ppermute | solution.py:146
  95.0 22.9 %collective-permute-done.2.refs_2_ = bf16[2,512,128]{2,1,0:T(8,128)(2,1)S(1)} collective-permute-done((bf16[2,512,128]{2,1,0:T(8,128)(2,1)S(1)}, bf16[2,512,128]{2,1,0:T(8,128)(2,1)S(1)}, u32[]{:S(2)}, u32[]{:S(2)}) %collective-permute-start.2) | collective-permute-done | bytes 262176 | tf_op jit(solution)/shard_map/ppermute | solution.py:145
  117.9 1.9 %collective-permute-start.3 = (bf16[2,512,128]{2,1,0:T(8,128)(2,1)S(1)}, bf16[2,512,128]{2,1,0:T(8,128)(2,1)S(1)}, u32[]{:S(2)}, u32[]{:S(2)}) collective-permute-start(bf16[2,512,128]{2,1,0:T(8,128)(2,1)S(1)} %collective-permute-done.2.refs_2_), channel_id=1, source_target_pairs={{0,32},{32,0},{1,33},{33,1},{2,34},{34,2},{3,35},{35,3},{4,36},{36... | collective-permute-start | bytes 786440 | tf_op jit(solution)/shard_map/ppermute | solution.py:146
  119.8 0.0 collective-permute-done.1.refs_1_
  119.8 1.5 collective-permute-done.3.refs_3_
  121.3 0.0 all-to-all-done.3.held
  121.3 1.2 first_contract.1
  122.5 4.6 %all-to-all-start.4 = ((bf16[32,2,16,128]{3,2,1,0:T(8,128)(2,1)}), bf16[32,2,16,128]{3,2,1,0:T(8,128)(2,1)S(1)}, u32[]{:S(2)}, u32[]{:S(2)}) async-start(bf16[32,2,16,128]{3,2,1,0:T(8,128)(2,1)} %bitcast.13), calls=%async_computation.4 | async-start | bytes 524288 | tf_op jit(solution)/shard_map/all_to_all | solution.py:136
  127.1 0.2 slice.79
  127.3 2.2 %collective-permute-start = (bf16[16,2,8,16,128]{4,3,2,1,0:T(8,128)(2,1)S(1)}, bf16[16,2,8,16,128]{4,3,2,1,0:T(8,128)(2,1)S(1)}, u32[]{:S(2)}, u32[]{:S(2)}) collective-permute-start(bf16[16,2,8,16,128]{4,3,2,1,0:T(8,128)(2,1)S(1)} %bitcast.22), channel_id=1, source_target_pairs={{0,32},{32,0},{1,33},{33,1},{2,34},{34,2},{3,35},{35,3},{4,36},{36... | collective-permute-start | bytes 3145736 | tf_op jit(solution)/shard_map/ppermute | solution.py:156
  129.5 2.4 %collective-permute-done.other = bf16[16,2,8,16,128]{4,3,2,1,0:T(8,128)(2,1)S(1)} collective-permute-done((bf16[16,2,8,16,128]{4,3,2,1,0:T(8,128)(2,1)S(1)}, bf16[16,2,8,16,128]{4,3,2,1,0:T(8,128)(2,1)S(1)}, u32[]{:S(2)}, u32[]{:S(2)}) %collective-permute-start) | collective-permute-done | bytes 1048608 | tf_op jit(solution)/shard_map/ppermute | solution.py:156
  131.9 6.8 %all-to-all-done.4.state = bf16[32,2,16,128]{3,2,1,0:T(8,128)(2,1)S(1)} async-done(((bf16[32,2,16,128]{3,2,1,0:T(8,128)(2,1)}), bf16[32,2,16,128]{3,2,1,0:T(8,128)(2,1)S(1)}, u32[]{:S(2)}, u32[]{:S(2)}) %all-to-all-start.4) | async-done | bytes 262176 | tf_op jit(solution)/shard_map/all_to_all | solution.py:136
  138.7 0.4 contract.2
  139.1 24.4 %all_to_all.30.state = bf16[32,2,16,128]{3,2,1,0:T(8,128)(2,1)S(1)} all-to-all(bf16[32,2,16,128]{3,2,1,0:T(8,128)(2,1)S(1)} %contract.2), channel_id=1, replica_groups=mesh['x'=4,'zh'=4,'core'=2,'za'=2,'zb'=4,'y'=4] {'za','zb','y'}, dimensions={0} | all-to-all | bytes 524288 | tf_op jit(solution)/shard_map/all_to_all | solution.py:136
  163.5 1.1 contract.3
  (8 shorter events, 0.1 us)
Async XLA Ops:
  0.0 19.5 %copy-start.1 = (s32[3]{0:T(128)S(1)}, s32[3]{0:T(128)}, u32[]{:S(2)}) copy-start(s32[3]{0:T(128)} %owners.1) | copy-start | bytes 40
  3.1 21.6 %all-to-all-start = ((bf16[8,16,128]{2,1,0:T(8,128)(2,1)}), bf16[8,16,128]{2,1,0:T(8,128)(2,1)S(1)}, u32[]{:S(2)}, u32[]{:S(2)}) async-start(bf16[8,16,128]{2,1,0:T(8,128)(2,1)} %branch_slice.1), calls=%async_computation | async-start | bytes 65536 | tf_op jit(solution)/shard_map/all_to_all | solution.py:136
  25.4 39.2 %all-to-all-start.1 = ((bf16[4,3,16,128]{3,2,1,0:T(8,128)(2,1)}), bf16[4,3,16,128]{3,2,1,0:T(8,128)(2,1)S(1)}, u32[]{:S(2)}, u32[]{:S(2)}) async-start(bf16[4,3,16,128]{3,2,1,0:T(8,128)(2,1)} %broadcast_in_dim.6), calls=%async_computation.1 | async-start | bytes 98304 | tf_op jit(solution)/shard_map/all_to_all | solution.py:136
  65.3 16.4 %all-to-all-start.2 = ((bf16[8,3,16,128]{3,2,1,0:T(8,128)(2,1)}), bf16[8,3,16,128]{3,2,1,0:T(8,128)(2,1)S(1)}, u32[]{:S(2)}, u32[]{:S(2)}) async-start(bf16[8,3,16,128]{3,2,1,0:T(8,128)(2,1)} %broadcast_in_dim.7), calls=%async_computation.2 | async-start | bytes 196608 | tf_op jit(solution)/shard_map/all_to_all | solution.py:136
  83.1 7.6 %copy-start = (bf16[2,512,128]{2,1,0:T(8,128)(2,1)S(1)}, bf16[2,512,128]{2,1,0:T(8,128)(2,1)}, u32[]{:S(2)}) copy-start(bf16[2,512,128]{2,1,0:T(8,128)(2,1)} %refs_0_.1) | copy-start | bytes 786436
  83.1 38.2 %all-to-all-start.3 = ((bf16[16,20,16,128]{3,2,1,0:T(8,128)(2,1)}), bf16[16,20,16,128]{3,2,1,0:T(8,128)(2,1)S(1)}, u32[]{:S(2)}, u32[]{:S(2)}) async-start(bf16[16,20,16,128]{3,2,1,0:T(8,128)(2,1)} %broadcast_in_dim.8), calls=%async_computation.3 | async-start | bytes 2621440 | tf_op jit(solution)/shard_map/all_to_all | solution.py:136
  90.7 27.2 %collective-permute-start.2 = (bf16[2,512,128]{2,1,0:T(8,128)(2,1)S(1)}, bf16[2,512,128]{2,1,0:T(8,128)(2,1)S(1)}, u32[]{:S(2)}, u32[]{:S(2)}) collective-permute-start(bf16[2,512,128]{2,1,0:T(8,128)(2,1)S(1)} %copy-done), channel_id=1, source_target_pairs={{0,16},{16,0},{1,17},{17,1},{2,18},{18,2},{3,19},{19,3},{4,20},{20... | collective-permute-start | bytes 786440 | tf_op jit(solution)/shard_map/ppermute | solution.py:145
  93.1 26.8 %collective-permute-start.1 = (bf16[2,512,128]{2,1,0:T(8,128)(2,1)S(1)}, bf16[2,512,128]{2,1,0:T(8,128)(2,1)S(1)}, u32[]{:S(2)}, u32[]{:S(2)}) collective-permute-start(bf16[2,512,128]{2,1,0:T(8,128)(2,1)S(1)} %copy-done), channel_id=1, source_target_pairs={{0,32},{32,0},{1,33},{33,1},{2,34},{34,2},{3,35},{35,3},{4,36},{36... | collective-permute-start | bytes 786440 | tf_op jit(solution)/shard_map/ppermute | solution.py:146
  117.9 3.4 %collective-permute-start.3 = (bf16[2,512,128]{2,1,0:T(8,128)(2,1)S(1)}, bf16[2,512,128]{2,1,0:T(8,128)(2,1)S(1)}, u32[]{:S(2)}, u32[]{:S(2)}) collective-permute-start(bf16[2,512,128]{2,1,0:T(8,128)(2,1)S(1)} %collective-permute-done.2.refs_2_), channel_id=1, source_target_pairs={{0,32},{32,0},{1,33},{33,1},{2,34},{34,2},{3,35},{35,3},{4,36},{36... | collective-permute-start | bytes 786440 | tf_op jit(solution)/shard_map/ppermute | solution.py:146
  122.5 16.2 %all-to-all-start.4 = ((bf16[32,2,16,128]{3,2,1,0:T(8,128)(2,1)}), bf16[32,2,16,128]{3,2,1,0:T(8,128)(2,1)S(1)}, u32[]{:S(2)}, u32[]{:S(2)}) async-start(bf16[32,2,16,128]{3,2,1,0:T(8,128)(2,1)} %bitcast.13), calls=%async_computation.4 | async-start | bytes 524288 | tf_op jit(solution)/shard_map/all_to_all | solution.py:136
  127.3 4.6 %collective-permute-start = (bf16[16,2,8,16,128]{4,3,2,1,0:T(8,128)(2,1)S(1)}, bf16[16,2,8,16,128]{4,3,2,1,0:T(8,128)(2,1)S(1)}, u32[]{:S(2)}, u32[]{:S(2)}) collective-permute-start(bf16[16,2,8,16,128]{4,3,2,1,0:T(8,128)(2,1)S(1)} %bitcast.22), channel_id=1, source_target_pairs={{0,32},{32,0},{1,33},{33,1},{2,34},{34,2},{3,35},{35,3},{4,36},{36... | collective-permute-start | bytes 3145736 | tf_op jit(solution)/shard_map/ppermute | solution.py:156

commit v3 on v2

--- a/solution.py
+++ b/solution.py
@@ -1,3 +1,5 @@
+import functools
+
 import jax
 import jax.numpy as jnp
 from jax import lax
@@ -19,7 +21,7 @@
     return (lax.axis_index("x") * 4 + lax.axis_index("zh")) * 2 + lax.axis_index("core")
 
 
-def slice_kernel(owners, slices, relabels, left, right, out):
+def slice_kernel(owners, slices, relabels, left, right, out, l_own, r_own, sems):
     row = own_row()
     used = [owners[k] == row for k in range(3)]
     chosen = jnp.int32(0)
@@ -28,12 +30,14 @@
     at_z, at_y = lax.axis_index("za") * 4 + lax.axis_index("zb"), lax.axis_index("y")
     block = jnp.where(used[0], at_z * 4 + at_y, at_y * 8 + at_z)
     rows = pl.ds(pl.multiple_of(block * 16, 16), 16)
-    both = jnp.concatenate([left[0, 0, rows, :], left[0, 1, rows, :]], axis=0)
-    by_real = jnp.dot(both, right[0, chosen, 0], preferred_element_type=F32)
-    by_imag = jnp.dot(both, right[0, chosen, 1], preferred_element_type=F32)
-    real = by_real[:16] - by_imag[16:]
-    imag = by_imag[:16] + by_real[16:]
-    branch = jnp.concatenate([real, imag], axis=0).astype(BF16)
+    copies = [
+        pltpu.make_async_copy(right.at[0, chosen, 0], r_own.at[0], sems.at[0]),
+        pltpu.make_async_copy(right.at[0, chosen, 1], r_own.at[1], sems.at[1]),
+        pltpu.make_async_copy(left.at[0, 0, rows], l_own.at[0], sems.at[2]),
+        pltpu.make_async_copy(left.at[0, 1, rows], l_own.at[1], sems.at[3]),
+    ]
+    for copy in copies:
+        copy.start()
     q = lax.broadcasted_iota(jnp.int32, (512, 512), 0)
     arrived = (((q >> 3) & 1) << 8) | (((q >> 4) & 15) << 4) | (((q >> 8) & 1) << 3) | (q & 7)
     place = jnp.where(used[1], arrived, q)
@@ -41,6 +45,14 @@
     mapping = jnp.where(used[1], relabels[0:1, :], mapping)
     mapping = jnp.where(used[2], relabels[1:2, :], mapping)
     onehot = jnp.where(place == mapping, 1.0, 0.0).astype(BF16)
+    for copy in copies:
+        copy.wait()
+    both = jnp.concatenate([l_own[0], l_own[1]], axis=0)
+    by_real = jnp.dot(both, r_own[0], preferred_element_type=F32)
+    by_imag = jnp.dot(both, r_own[1], preferred_element_type=F32)
+    real = by_real[:16] - by_imag[16:]
+    imag = by_imag[:16] + by_real[16:]
+    branch = jnp.concatenate([real, imag], axis=0).astype(BF16)
     moved = lax.dot_general(branch, onehot, (((1,), (1,)), ((), ())), preferred_element_type=F32)
     halves = jnp.concatenate([moved[:8], moved[16:24], moved[8:16], moved[24:]], axis=0)
     moved = jnp.where(used[0], halves, moved).astype(BF16)
@@ -50,6 +62,7 @@
 
 
 VMEM = pl.BlockSpec(memory_space=pltpu.VMEM)
+HBM = pl.BlockSpec(memory_space=pl.ANY)
 SMEM = pl.BlockSpec(memory_space=pltpu.SMEM)
 SMALL = pltpu.CompilerParams(vmem_limit_bytes=16 << 20)
 
@@ -57,11 +70,54 @@
 def branch_slice(owners, slices, relabels, left, right):
     return pl.pallas_call(
         slice_kernel,
-        in_specs=[SMEM, SMEM, VMEM, VMEM, VMEM],
-        out_specs=VMEM,
+        in_specs=[SMEM, SMEM, VMEM, HBM, HBM],
+        out_specs=VMEM,
+        scratch_shapes=[
+            pltpu.VMEM((2, 16, 512), BF16),
+            pltpu.VMEM((2, 512, 512), BF16),
+            pltpu.SemaphoreType.DMA((4,)),
+        ],
         out_shape=jax.ShapeDtypeStruct((8, *TILE), BF16),
         name="branch_slice",
     )(owners, slices, relabels, left, right)
+
+
+def pick_kernel(by_zh, owners, tiles, out):
+    for k in range(3):
+        at_x, at_zh, at_core = owners[k] >> 3, (owners[k] >> 1) & 3, owners[k] & 1
+        tile = tiles[at_zh, k] if by_zh else tiles[at_x * 2 + at_core]
+        for i in range(out.shape[0]):
+            out[i, k] = tile
+
+
+def pick(owners, tiles, by_zh, count):
+    return pl.pallas_call(
+        functools.partial(pick_kernel, by_zh),
+        in_specs=[SMEM, VMEM],
+        out_specs=VMEM,
+        out_shape=jax.ShapeDtypeStruct((count, 3, *TILE), BF16),
+        compiler_params=SMALL,
+        name="pick",
+    )(owners, tiles)
+
+
+def pack_kernel(tiles, out):
+    half = lax.axis_index("za") * 4
+    for j in range(20):
+        tile = tiles[half + j, 0] if j < 4 else tiles[(j - 4) % 8, 1 + (j - 4) // 8]
+        for i in range(16):
+            out[i, j] = tile
+
+
+def pack(tiles):
+    return pl.pallas_call(
+        pack_kernel,
+        in_specs=[VMEM],
+        out_specs=VMEM,
+        out_shape=jax.ShapeDtypeStruct((16, 20, *TILE), BF16),
+        compiler_params=SMALL,
+        name="pack",
+    )(tiles)
 
 
 def first_kernel(held, *refs):
@@ -136,22 +192,19 @@
     return lax.all_to_all(blocks, axes, 0, 0, tiled=True)
 
 
-def to_all(block, axes, count):
-    return send(jnp.broadcast_to(block[None], (count, *block.shape)), axes)
-
-
-def body(stem, left, right, owners, slices, relabels):
-    at_x, at_zh, at_core = owners // 8, (owners // 2) % 4, owners % 2
+def steps(stem, left, right, owners, slices, relabels):
     across = lax.ppermute(stem, "za", FLIP)
-    stems = (stem, lax.ppermute(stem, "core", FLIP), across, lax.ppermute(across, "core", FLIP))
-    tiles = send(branch_slice(owners, slices, relabels, left, right), SPREAD)
-    mine = [lax.dynamic_index_in_dim(tiles, at_x[k] * 2 + at_core[k], 0, keepdims=False) for k in range(3)]
-    shares = to_all(jnp.stack(mine), "zh", 4)
-    shares = jnp.stack([lax.dynamic_index_in_dim(shares, at_zh[k], 0, keepdims=False)[k] for k in range(3)])
-    shares = to_all(shares, LINE, 8)
-    first = lax.dynamic_slice_in_dim(shares[:, 0], lax.axis_index("za") * 4, 4, 0)
-    held = to_all(jnp.concatenate([first, shares[:, 1], shares[:, 2]]), PLANE, 16)
-    state = first_contract(held, stems).reshape(32, 2, *TILE)
+    beside = lax.ppermute(stem, "core", FLIP)
+    both = lax.ppermute(across, "core", FLIP)
+    made = branch_slice(owners, slices, relabels, left, right)
+    tiles = send(made, SPREAD)
+    picked = pick(owners, tiles, False, 4)
+    shares = send(picked, "zh")
+    picked = pick(owners, shares, True, 8)
+    shares = send(picked, LINE)
+    packed = pack(shares)
+    held = send(packed, PLANE)
+    state = first_contract(held, (stem, beside, across, both)).reshape(32, 2, *TILE)
     own = held[:, 4:].reshape(16, 2, 8, *TILE)
     other = lax.ppermute(own, "core", FLIP)
     state = contract(own, other, send(state, NEAR), (32, 2, *TILE), 0)
@@ -168,4 +221,4 @@
         P(),
         P(),
     )
-    return jax.shard_map(body, mesh=fine, in_specs=in_specs, out_specs=P(None, None, ALL), check_vma=False)
+    return jax.shard_map(steps, mesh=fine, in_specs=in_specs, out_specs=P(None, None, ALL), check_vma=False)

time: 165 us -> 163 us (0.988)
  blocking collectives: 24.4 us -> 100 us
  starting transfers between devices: 59 us -> 19.7 us
  waiting for transfers between devices: 61.6 us -> 33.8 us
  between operations: 9.64 us -> 0.1 us
  local copies, waits for them, and re-layouts: 4.17 us -> 0.19 us
  Pallas kernels: 5.83 us -> 8.35 us
    all_to_all x1 -> x4, blocking collectives: 24.4 us -> 100 us  [send(): return lax.all_to_all(blocks, axes, 0, 0, tiled=True)]
    all_to_all x5 -> x2, starting transfers between devices: 50.6 us -> 11.3 us  [send(): return lax.all_to_all(blocks, axes, 0, 0, tiled=True)]
    all_to_all x5 -> x2, waiting for transfers between devices: 34.8 us -> 6.8 us  [send(): return lax.all_to_all(blocks, axes, 0, 0, tiled=True)]
    broadcast_in_dim x3 -> x0, local copies, waits for them, and re-layouts: 2.62 us -> none  [to_all(): return send(jnp.broadcast_to(block[None], (count, *block.shape)), axes)]
    pallas_call x1 -> x4, Pallas kernels: 3.09 us -> 5.61 us  [the longest x1 3.16 us: branch_slice(): pl.pallas_call(slice_kernel, in_specs=[SMEM, SMEM, VMEM, HBM, HBM], out_s...]
  transfers between devices with their start and end apart: 9 -> 6, of which waited for: 6 -> 4; matrix products, arithmetic and copies ran while one was open for 1% -> 0% of each run, Pallas kernels for 0% -> 0%
where the time goes in v3:
time: 163 us; the launch traced here: 162 us
  blocking collectives  100 us (61%)
  waiting for transfers between devices  33.8 us (21%)
  starting transfers between devices  19.7 us (12%)
  Pallas kernels  8.35 us (5%)
    all_to_all x4, blocking collectives, send(): return lax.all_to_all(blocks, axes, 0, 0, tiled=True)  100 us
    ppermute x1, waiting for transfers between devices, steps(): across = lax.ppermute(stem, 'za', FLIP)  23.2 us
    all_to_all x2, starting transfers between devices, send(): return lax.all_to_all(blocks, axes, 0, 0, tiled=True)  11.3 us
    all_to_all x2, waiting for transfers between devices, send(): return lax.all_to_all(blocks, axes, 0, 0, tiled=True)  6.8 us
  transfers between devices with their start and end apart: 6, of which 4 were waited for; matrix products, arithmetic and copies ran while one was open for 0% of the time, Pallas kernels for 0%

profile of v3, /device:TPU:2, one launch (start us, length us, event | category | flops | bytes accessed | tf_op | source)
XLA Modules:
  0.0 162.2 jit_solution(6700752210470778540)
XLA Ops:
  0.0 0.0 copy-start.1
  0.0 3.2 %branch_slice.1 = bf16[8,16,128]{2,1,0:T(8,128)(2,1)} custom-call(s32[3]{0:T(128)} %owners.5, s32[3]{0:T(128)} %slices.1, s32[2,512]{1,0:T(2,128)} %relabels.1, bf16[1,2,512,512]{3,2,1,0:T(8,128)(2,1)} %left.1, bf16[1,2,2,512,512]{4,3,2,1,0:T(8,128)(2,1)} %right.1), custom_call_target="tpu_custom_call" | custom-call | tf_op jit(solution)/shard_map/branch_slice/pallas_call | solution.py:71
  3.2 20.4 %all_to_all.30.tiles = bf16[8,16,128]{2,1,0:T(8,128)(2,1)S(1)} all-to-all(bf16[8,16,128]{2,1,0:T(8,128)(2,1)} %branch_slice.1), channel_id=1, replica_groups=mesh['x'=4,'zh'=4,'core'=2,'za'=2,'zb'=4,'y'=4] {'x','core'}, dimensions={0} | all-to-all | bytes 65536 | tf_op jit(solution)/shard_map/all_to_all | solution.py:192
  23.6 0.0 copy-done.1
  23.6 0.6 pick.2
  24.1 39.1 %all_to_all.31.tiles = bf16[4,3,16,128]{3,2,1,0:T(8,128)(2,1)S(1)} all-to-all(bf16[4,3,16,128]{3,2,1,0:T(8,128)(2,1)S(1)} %pick.2), channel_id=1, replica_groups=mesh['x'=4,'zh'=4,'core'=2,'za'=2,'zb'=4,'y'=4] {'zh'}, dimensions={0} | all-to-all | bytes 98304 | tf_op jit(solution)/shard_map/all_to_all | solution.py:192
  63.2 0.6 pick.3
  63.8 16.0 %all_to_all.32.tiles = bf16[8,3,16,128]{3,2,1,0:T(8,128)(2,1)S(1)} all-to-all(bf16[8,3,16,128]{3,2,1,0:T(8,128)(2,1)S(1)} %pick.3), channel_id=1, replica_groups=mesh['x'=4,'zh'=4,'core'=2,'za'=2,'zb'=4,'y'=4] {'za','zb'}, dimensions={0} | all-to-all | bytes 196608 | tf_op jit(solution)/shard_map/all_to_all | solution.py:192
  79.8 1.3 pack.1
  81.1 0.0 copy-start
  81.1 6.7 %all-to-all-start.3 = ((bf16[16,20,16,128]{3,2,1,0:T(8,128)(2,1)}), bf16[16,20,16,128]{3,2,1,0:T(8,128)(2,1)S(1)}, u32[]{:S(2)}, u32[]{:S(2)}) async-start(bf16[16,20,16,128]{3,2,1,0:T(8,128)(2,1)} %pack.1), calls=%async_computation.3 | async-start | bytes 2621440 | tf_op jit(solution)/shard_map/all_to_all | solution.py:192
  87.8 0.0 copy-done
  87.8 2.3 %collective-permute-start.2 = (bf16[2,512,128]{2,1,0:T(8,128)(2,1)S(1)}, bf16[2,512,128]{2,1,0:T(8,128)(2,1)S(1)}, u32[]{:S(2)}, u32[]{:S(2)}) collective-permute-start(bf16[2,512,128]{2,1,0:T(8,128)(2,1)S(1)} %copy-done), channel_id=1, source_target_pairs={{0,16},{16,0},{1,17},{17,1},{2,18},{18,2},{3,19},{19,3},{4,20},{20... | collective-permute-start | bytes 786440 | tf_op jit(solution)/shard_map/ppermute | solution.py:196
  90.1 1.9 %collective-permute-start.1 = (bf16[2,512,128]{2,1,0:T(8,128)(2,1)S(1)}, bf16[2,512,128]{2,1,0:T(8,128)(2,1)S(1)}, u32[]{:S(2)}, u32[]{:S(2)}) collective-permute-start(bf16[2,512,128]{2,1,0:T(8,128)(2,1)S(1)} %copy-done), channel_id=1, source_target_pairs={{0,32},{32,0},{1,33},{33,1},{2,34},{34,2},{3,35},{35,3},{4,36},{36... | collective-permute-start | bytes 786440 | tf_op jit(solution)/shard_map/ppermute | solution.py:197
  92.0 23.2 %collective-permute-done.2.refs_2_ = bf16[2,512,128]{2,1,0:T(8,128)(2,1)S(1)} collective-permute-done((bf16[2,512,128]{2,1,0:T(8,128)(2,1)S(1)}, bf16[2,512,128]{2,1,0:T(8,128)(2,1)S(1)}, u32[]{:S(2)}, u32[]{:S(2)}) %collective-permute-start.2) | collective-permute-done | bytes 262176 | tf_op jit(solution)/shard_map/ppermute | solution.py:196
  115.2 1.9 %collective-permute-start.3 = (bf16[2,512,128]{2,1,0:T(8,128)(2,1)S(1)}, bf16[2,512,128]{2,1,0:T(8,128)(2,1)S(1)}, u32[]{:S(2)}, u32[]{:S(2)}) collective-permute-start(bf16[2,512,128]{2,1,0:T(8,128)(2,1)S(1)} %collective-permute-done.2.refs_2_), channel_id=1, source_target_pairs={{0,32},{32,0},{1,33},{33,1},{2,34},{34,2},{3,35},{35,3},{4,36},{36... | collective-permute-start | bytes 786440 | tf_op jit(solution)/shard_map/ppermute | solution.py:198
  117.1 0.0 collective-permute-done.1.refs_1_
  117.1 1.5 collective-permute-done.3.refs_3_
  118.6 0.0 all-to-all-done.3.held
  118.6 1.2 first_contract.1
  119.8 4.6 %all-to-all-start.4 = ((bf16[32,2,16,128]{3,2,1,0:T(8,128)(2,1)}), bf16[32,2,16,128]{3,2,1,0:T(8,128)(2,1)S(1)}, u32[]{:S(2)}, u32[]{:S(2)}) async-start(bf16[32,2,16,128]{3,2,1,0:T(8,128)(2,1)} %bitcast.1), calls=%async_computation.4 | async-start | bytes 524288 | tf_op jit(solution)/shard_map/all_to_all | solution.py:192
  124.4 0.2 slice.4
  124.6 2.2 %collective-permute-start = (bf16[16,2,8,16,128]{4,3,2,1,0:T(8,128)(2,1)S(1)}, bf16[16,2,8,16,128]{4,3,2,1,0:T(8,128)(2,1)S(1)}, u32[]{:S(2)}, u32[]{:S(2)}) collective-permute-start(bf16[16,2,8,16,128]{4,3,2,1,0:T(8,128)(2,1)S(1)} %bitcast.2), channel_id=1, source_target_pairs={{0,32},{32,0},{1,33},{33,1},{2,34},{34,2},{3,35},{35,3},{4,36},{36... | collective-permute-start | bytes 3145736 | tf_op jit(solution)/shard_map/ppermute | solution.py:209
  126.8 2.4 %collective-permute-done.other = bf16[16,2,8,16,128]{4,3,2,1,0:T(8,128)(2,1)S(1)} collective-permute-done((bf16[16,2,8,16,128]{4,3,2,1,0:T(8,128)(2,1)S(1)}, bf16[16,2,8,16,128]{4,3,2,1,0:T(8,128)(2,1)S(1)}, u32[]{:S(2)}, u32[]{:S(2)}) %collective-permute-start) | collective-permute-done | bytes 1048608 | tf_op jit(solution)/shard_map/ppermute | solution.py:209
  129.2 6.8 %all-to-all-done.4.state = bf16[32,2,16,128]{3,2,1,0:T(8,128)(2,1)S(1)} async-done(((bf16[32,2,16,128]{3,2,1,0:T(8,128)(2,1)}), bf16[32,2,16,128]{3,2,1,0:T(8,128)(2,1)S(1)}, u32[]{:S(2)}, u32[]{:S(2)}) %all-to-all-start.4) | async-done | bytes 262176 | tf_op jit(solution)/shard_map/all_to_all | solution.py:192
  136.0 0.4 contract.2
  136.4 24.7 %all_to_all.33.state = bf16[32,2,16,128]{3,2,1,0:T(8,128)(2,1)S(1)} all-to-all(bf16[32,2,16,128]{3,2,1,0:T(8,128)(2,1)S(1)} %contract.2), channel_id=1, replica_groups=mesh['x'=4,'zh'=4,'core'=2,'za'=2,'zb'=4,'y'=4] {'za','zb','y'}, dimensions={0} | all-to-all | bytes 524288 | tf_op jit(solution)/shard_map/all_to_all | solution.py:192
  161.1 1.1 contract.3
Async XLA Ops:
  0.0 23.6 %copy-start.1 = (s32[3]{0:T(128)S(1)}, s32[3]{0:T(128)}, u32[]{:S(2)}) copy-start(s32[3]{0:T(128)} %owners.5) | copy-start | bytes 40
  81.1 6.7 %copy-start = (bf16[2,512,128]{2,1,0:T(8,128)(2,1)S(1)}, bf16[2,512,128]{2,1,0:T(8,128)(2,1)}, u32[]{:S(2)}) copy-start(bf16[2,512,128]{2,1,0:T(8,128)(2,1)} %refs_0_.1) | copy-start | bytes 786436
  81.1 37.5 %all-to-all-start.3 = ((bf16[16,20,16,128]{3,2,1,0:T(8,128)(2,1)}), bf16[16,20,16,128]{3,2,1,0:T(8,128)(2,1)S(1)}, u32[]{:S(2)}, u32[]{:S(2)}) async-start(bf16[16,20,16,128]{3,2,1,0:T(8,128)(2,1)} %pack.1), calls=%async_computation.3 | async-start | bytes 2621440 | tf_op jit(solution)/shard_map/all_to_all | solution.py:192
  87.8 27.4 %collective-permute-start.2 = (bf16[2,512,128]{2,1,0:T(8,128)(2,1)S(1)}, bf16[2,512,128]{2,1,0:T(8,128)(2,1)S(1)}, u32[]{:S(2)}, u32[]{:S(2)}) collective-permute-start(bf16[2,512,128]{2,1,0:T(8,128)(2,1)S(1)} %copy-done), channel_id=1, source_target_pairs={{0,16},{16,0},{1,17},{17,1},{2,18},{18,2},{3,19},{19,3},{4,20},{20... | collective-permute-start | bytes 786440 | tf_op jit(solution)/shard_map/ppermute | solution.py:196
  90.1 27.0 %collective-permute-start.1 = (bf16[2,512,128]{2,1,0:T(8,128)(2,1)S(1)}, bf16[2,512,128]{2,1,0:T(8,128)(2,1)S(1)}, u32[]{:S(2)}, u32[]{:S(2)}) collective-permute-start(bf16[2,512,128]{2,1,0:T(8,128)(2,1)S(1)} %copy-done), channel_id=1, source_target_pairs={{0,32},{32,0},{1,33},{33,1},{2,34},{34,2},{3,35},{35,3},{4,36},{36... | collective-permute-start | bytes 786440 | tf_op jit(solution)/shard_map/ppermute | solution.py:197
  115.2 3.4 %collective-permute-start.3 = (bf16[2,512,128]{2,1,0:T(8,128)(2,1)S(1)}, bf16[2,512,128]{2,1,0:T(8,128)(2,1)S(1)}, u32[]{:S(2)}, u32[]{:S(2)}) collective-permute-start(bf16[2,512,128]{2,1,0:T(8,128)(2,1)S(1)} %collective-permute-done.2.refs_2_), channel_id=1, source_target_pairs={{0,32},{32,0},{1,33},{33,1},{2,34},{34,2},{3,35},{35,3},{4,36},{36... | collective-permute-start | bytes 786440 | tf_op jit(solution)/shard_map/ppermute | solution.py:198
  119.8 16.2 %all-to-all-start.4 = ((bf16[32,2,16,128]{3,2,1,0:T(8,128)(2,1)}), bf16[32,2,16,128]{3,2,1,0:T(8,128)(2,1)S(1)}, u32[]{:S(2)}, u32[]{:S(2)}) async-start(bf16[32,2,16,128]{3,2,1,0:T(8,128)(2,1)} %bitcast.1), calls=%async_computation.4 | async-start | bytes 524288 | tf_op jit(solution)/shard_map/all_to_all | solution.py:192
  124.6 4.6 %collective-permute-start = (bf16[16,2,8,16,128]{4,3,2,1,0:T(8,128)(2,1)S(1)}, bf16[16,2,8,16,128]{4,3,2,1,0:T(8,128)(2,1)S(1)}, u32[]{:S(2)}, u32[]{:S(2)}) collective-permute-start(bf16[16,2,8,16,128]{4,3,2,1,0:T(8,128)(2,1)S(1)} %bitcast.2), channel_id=1, source_target_pairs={{0,32},{32,0},{1,33},{33,1},{2,34},{34,2},{3,35},{35,3},{4,36},{36... | collective-permute-start | bytes 3145736 | tf_op jit(solution)/shard_map/ppermute | solution.py:209

commit v4 on v3

--- a/solution.py
+++ b/solution.py
@@ -29,6 +29,7 @@
         chosen = jnp.where(used[k], slices[k], chosen)
     at_z, at_y = lax.axis_index("za") * 4 + lax.axis_index("zb"), lax.axis_index("y")
     block = jnp.where(used[0], at_z * 4 + at_y, at_y * 8 + at_z)
+    block = jnp.where(used[2], (at_z >> 1) * 8 + at_y * 2 + (at_z & 1), block)
     rows = pl.ds(pl.multiple_of(block * 16, 16), 16)
     copies = [
         pltpu.make_async_copy(right.at[0, chosen, 0], r_own.at[0], sems.at[0]),
@@ -103,10 +104,14 @@
 
 def pack_kernel(tiles, out):
     half = lax.axis_index("za") * 4
-    for j in range(20):
-        tile = tiles[half + j, 0] if j < 4 else tiles[(j - 4) % 8, 1 + (j - 4) // 8]
+    for j in range(12):
+        tile = tiles[half + j, 0] if j < 4 else tiles[j - 4, 1]
         for i in range(16):
             out[i, j] = tile
+    for j in range(8):
+        tile = tiles[j, 2]
+        for x in range(4):
+            out[x * 4 + j // 2, 12 + j % 2] = tile
 
 
 def pack(tiles):
@@ -114,7 +119,7 @@
         pack_kernel,
         in_specs=[VMEM],
         out_specs=VMEM,
-        out_shape=jax.ShapeDtypeStruct((16, 20, *TILE), BF16),
+        out_shape=jax.ShapeDtypeStruct((16, 14, *TILE), BF16),
         compiler_params=SMALL,
         name="pack",
     )(tiles)
@@ -153,11 +158,20 @@
     )(held, *stems)
 
 
-def make_contract_kernel(pick):
+def make_contract_kernel(shifted):
     def kernel(own, other, state, out):
+        at_y = lax.axis_index("y")
         parts = []
         for ref in (own, other):
-            columns = [ref[c * 4 : c * 4 + 4, pick].reshape(512, 128) for c in range(4)]
+            if shifted:
+                columns = [
+                    jnp.concatenate(
+                        [ref[(at_y - y) & 3, c * 4 : c * 4 + 4].reshape(128, 128) for y in range(4)], axis=0
+                    )
+                    for c in range(4)
+                ]
+            else:
+                columns = [ref[c * 4 : c * 4 + 4].reshape(512, 128) for c in range(4)]
             parts.append(jnp.concatenate(columns, axis=1))
         both = jnp.concatenate([state[:, 0].reshape(512, 128), state[:, 1].reshape(512, 128)], axis=1)
         by_own = jnp.dot(parts[0], both, preferred_element_type=F32)
@@ -177,9 +191,9 @@
     return kernel
 
 
-def contract(own, other, state, shape, pick):
-    return pl.pallas_call(
-        make_contract_kernel(pick),
+def contract(own, other, state, shape, shifted):
+    return pl.pallas_call(
+        make_contract_kernel(shifted),
         in_specs=[VMEM] * 3,
         out_specs=VMEM,
         out_shape=jax.ShapeDtypeStruct(shape, BF16),
@@ -205,10 +219,17 @@
     packed = pack(shares)
     held = send(packed, PLANE)
     state = first_contract(held, (stem, beside, across, both)).reshape(32, 2, *TILE)
-    own = held[:, 4:].reshape(16, 2, 8, *TILE)
+    state = send(state, NEAR)
+    own, last = held[:, 4:12], held[:, 12:]
     other = lax.ppermute(own, "core", FLIP)
-    state = contract(own, other, send(state, NEAR), (32, 2, *TILE), 0)
-    return contract(own, other, send(state, COL), (2, 512, 128), 1)
+    state = contract(own, other, state, (32, 2, *TILE), False)
+    state = send(state, COL)
+    pieces = [last]
+    for offset in (1, 2, 3):
+        pieces.append(lax.ppermute(last, "y", [(i, (i + offset) % 4) for i in range(4)]))
+    last = jnp.stack(pieces)
+    other = lax.ppermute(last, "core", FLIP)
+    return contract(last, other, state, (2, 512, 128), True)
 
 
 def solution(mesh):

time: 163 us -> 164 us (level)
  the two profiles are of different devices: /device:TPU:2 before, /device:TPU:1 now
where the time goes in v4:
time: 164 us; the launch traced here: 163 us
  blocking collectives  75.2 us (46%)
  starting transfers between devices  42.8 us (26%)
  waiting for transfers between devices  36.2 us (22%)
  Pallas kernels  8.75 us (5%)
    all_to_all x3, blocking collectives, send(): return lax.all_to_all(blocks, axes, 0, 0, tiled=True)  75.2 us
    ppermute x1, waiting for transfers between devices, steps(): across = lax.ppermute(stem, 'za', FLIP)  22.9 us
    all_to_all x3, starting transfers between devices, send(): return lax.all_to_all(blocks, axes, 0, 0, tiled=True)  15.5 us
    ppermute x3, starting transfers between devices, steps(): lax.ppermute(last, 'y', [(i, (i + offset) % 4) for i in range(4)])  11.1 us
    all_to_all x3, waiting for transfers between devices, send(): return lax.all_to_all(blocks, axes, 0, 0, tiled=True)  6.96 us
    ppermute x1, starting transfers between devices, steps(): beside = lax.ppermute(stem, 'core', FLIP)  5.07 us
    ppermute x1, starting transfers between devices, steps(): other = lax.ppermute(last, 'core', FLIP)  4.34 us
  transfers between devices with their start and end apart: 11, of which 7 were waited for; matrix products, arithmetic and copies ran while one was open for 0% of the time, Pallas kernels for 0%

profile of v4, /device:TPU:1, one launch (start us, length us, event | category | flops | bytes accessed | tf_op | source)
XLA Modules:
  0.0 163.3 jit_solution(7385579716356169382)
XLA Ops:
  0.0 0.0 copy-start.1
  0.0 3.2 %branch_slice.1 = bf16[8,16,128]{2,1,0:T(8,128)(2,1)} custom-call(s32[3]{0:T(128)} %owners.5, s32[3]{0:T(128)} %slices.1, s32[2,512]{1,0:T(2,128)} %relabels.1, bf16[1,2,512,512]{3,2,1,0:T(8,128)(2,1)} %left.1, bf16[1,2,2,512,512]{4,3,2,1,0:T(8,128)(2,1)} %right.1), custom_call_target="tpu_custom_call" | custom-call | tf_op jit(solution)/shard_map/branch_slice/pallas_call | solution.py:72
  3.2 0.0 copy-start
  3.2 22.2 %all_to_all.30.tiles = bf16[8,16,128]{2,1,0:T(8,128)(2,1)S(1)} all-to-all(bf16[8,16,128]{2,1,0:T(8,128)(2,1)} %branch_slice.1), channel_id=1, replica_groups=mesh['x'=4,'zh'=4,'core'=2,'za'=2,'zb'=4,'y'=4] {'x','core'}, dimensions={0} | all-to-all | bytes 65536 | tf_op jit(solution)/shard_map/all_to_all | solution.py:206
  25.4 0.0 copy-done.1
  25.4 0.6 pick.2
  26.0 38.2 %all_to_all.31.tiles = bf16[4,3,16,128]{3,2,1,0:T(8,128)(2,1)S(1)} all-to-all(bf16[4,3,16,128]{3,2,1,0:T(8,128)(2,1)S(1)} %pick.2), channel_id=1, replica_groups=mesh['x'=4,'zh'=4,'core'=2,'za'=2,'zb'=4,'y'=4] {'zh'}, dimensions={0} | all-to-all | bytes 98304 | tf_op jit(solution)/shard_map/all_to_all | solution.py:206
  64.1 0.6 pick.3
  64.7 14.9 %all_to_all.32.tiles = bf16[8,3,16,128]{3,2,1,0:T(8,128)(2,1)S(1)} all-to-all(bf16[8,3,16,128]{3,2,1,0:T(8,128)(2,1)S(1)} %pick.3), channel_id=1, replica_groups=mesh['x'=4,'zh'=4,'core'=2,'za'=2,'zb'=4,'y'=4] {'za','zb'}, dimensions={0} | all-to-all | bytes 196608 | tf_op jit(solution)/shard_map/all_to_all | solution.py:206
  79.5 1.0 pack.1
  80.6 4.9 %all-to-all-start.3 = ((bf16[16,14,16,128]{3,2,1,0:T(8,128)(2,1)}), bf16[16,14,16,128]{3,2,1,0:T(8,128)(2,1)S(1)}, u32[]{:S(2)}, u32[]{:S(2)}) async-start(bf16[16,14,16,128]{3,2,1,0:T(8,128)(2,1)} %pack.1), calls=%async_computation.3 | async-start | bytes 1835008 | tf_op jit(solution)/shard_map/all_to_all | solution.py:206
  85.5 0.0 copy-done
  85.5 2.2 %collective-permute-start.6 = (bf16[2,512,128]{2,1,0:T(8,128)(2,1)S(1)}, bf16[2,512,128]{2,1,0:T(8,128)(2,1)S(1)}, u32[]{:S(2)}, u32[]{:S(2)}) collective-permute-start(bf16[2,512,128]{2,1,0:T(8,128)(2,1)S(1)} %copy-done), channel_id=1, source_target_pairs={{0,16},{16,0},{1,17},{17,1},{2,18},{18,2},{3,19},{19,3},{4,20},{20... | collective-permute-start | bytes 786440 | tf_op jit(solution)/shard_map/ppermute | solution.py:210
  87.7 5.1 %collective-permute-start.5 = (bf16[2,512,128]{2,1,0:T(8,128)(2,1)S(1)}, bf16[2,512,128]{2,1,0:T(8,128)(2,1)S(1)}, u32[]{:S(2)}, u32[]{:S(2)}) collective-permute-start(bf16[2,512,128]{2,1,0:T(8,128)(2,1)S(1)} %copy-done), channel_id=1, source_target_pairs={{0,32},{32,0},{1,33},{33,1},{2,34},{34,2},{3,35},{35,3},{4,36},{36... | collective-permute-start | bytes 786440 | tf_op jit(solution)/shard_map/ppermute | solution.py:211
  92.8 22.9 %collective-permute-done.6.refs_2_ = bf16[2,512,128]{2,1,0:T(8,128)(2,1)S(1)} collective-permute-done((bf16[2,512,128]{2,1,0:T(8,128)(2,1)S(1)}, bf16[2,512,128]{2,1,0:T(8,128)(2,1)S(1)}, u32[]{:S(2)}, u32[]{:S(2)}) %collective-permute-start.6) | collective-permute-done | bytes 262176 | tf_op jit(solution)/shard_map/ppermute | solution.py:210
  115.8 2.4 %collective-permute-start.7 = (bf16[2,512,128]{2,1,0:T(8,128)(2,1)S(1)}, bf16[2,512,128]{2,1,0:T(8,128)(2,1)S(1)}, u32[]{:S(2)}, u32[]{:S(2)}) collective-permute-start(bf16[2,512,128]{2,1,0:T(8,128)(2,1)S(1)} %collective-permute-done.6.refs_2_), channel_id=1, source_target_pairs={{0,32},{32,0},{1,33},{33,1},{2,34},{34,2},{3,35},{35,3},{4,36},{36... | collective-permute-start | bytes 786440 | tf_op jit(solution)/shard_map/ppermute | solution.py:212
  118.2 0.0 collective-permute-done.5.refs_1_
  118.2 1.1 collective-permute-done.7.refs_3_
  119.3 0.0 all-to-all-done.3.held
  119.3 1.2 first_contract.1
  120.5 5.0 %all-to-all-start.4 = ((bf16[32,2,16,128]{3,2,1,0:T(8,128)(2,1)}), bf16[32,2,16,128]{3,2,1,0:T(8,128)(2,1)S(1)}, u32[]{:S(2)}, u32[]{:S(2)}) async-start(bf16[32,2,16,128]{3,2,1,0:T(8,128)(2,1)} %bitcast.4), calls=%async_computation.4 | async-start | bytes 524288 | tf_op jit(solution)/shard_map/all_to_all | solution.py:206
  125.5 2.1 %collective-permute-start.4 = (bf16[16,8,16,128]{3,2,1,0:T(8,128)(2,1)S(1)}, bf16[16,8,16,128]{3,2,1,0:T(8,128)(2,1)S(1)}, u32[]{:S(2)}, u32[]{:S(2)}) collective-permute-start(bf16[16,8,16,128]{3,2,1,0:T(8,128)(2,1)S(1)} %slice.9.own), channel_id=1, source_target_pairs={{0,32},{32,0},{1,33},{33,1},{2,34},{34,2},{3,35},{35,3},{4,36},{36... | collective-permute-start | bytes 1572872 | tf_op jit(solution)/shard_map/ppermute | solution.py:224
  127.6 1.7 %collective-permute-done.4.other = bf16[16,8,16,128]{3,2,1,0:T(8,128)(2,1)S(1)} collective-permute-done((bf16[16,8,16,128]{3,2,1,0:T(8,128)(2,1)S(1)}, bf16[16,8,16,128]{3,2,1,0:T(8,128)(2,1)S(1)}, u32[]{:S(2)}, u32[]{:S(2)}) %collective-permute-start.4) | collective-permute-done | bytes 524320 | tf_op jit(solution)/shard_map/ppermute | solution.py:224
  129.3 7.0 %all-to-all-done.4.state = bf16[32,2,16,128]{3,2,1,0:T(8,128)(2,1)S(1)} async-done(((bf16[32,2,16,128]{3,2,1,0:T(8,128)(2,1)}), bf16[32,2,16,128]{3,2,1,0:T(8,128)(2,1)S(1)}, u32[]{:S(2)}, u32[]{:S(2)}) %all-to-all-start.4) | async-done | bytes 262176 | tf_op jit(solution)/shard_map/all_to_all | solution.py:206
  136.2 1.1 contract.2
  137.4 5.6 %all-to-all-start.5 = ((bf16[32,2,16,128]{3,2,1,0:T(8,128)(2,1)}), bf16[32,2,16,128]{3,2,1,0:T(8,128)(2,1)S(1)}, u32[]{:S(2)}, u32[]{:S(2)}) async-start(bf16[32,2,16,128]{3,2,1,0:T(8,128)(2,1)} %contract.2), calls=%async_computation.5 | async-start | bytes 524288 | tf_op jit(solution)/shard_map/all_to_all | solution.py:206
  143.1 4.6 %collective-permute-start.1 = (bf16[16,2,16,128]{3,2,1,0:T(8,128)(2,1)S(1)}, bf16[16,2,16,128]{3,2,1,0:T(8,128)(2,1)S(1)}, u32[]{:S(2)}, u32[]{:S(2)}) collective-permute-start(bf16[16,2,16,128]{3,2,1,0:T(8,128)(2,1)S(1)} %get-tuple-element.6), channel_id=1, source_target_pairs={{0,2},{1,3},{2,0},{3,1},{4,6},{5,7},{6,4},{7,5},{8,10},{9,11},{10,... | collective-permute-start | bytes 393224 | tf_op jit(solution)/shard_map/ppermute | solution.py:229
  147.7 2.2 %collective-permute-start = (bf16[16,2,16,128]{3,2,1,0:T(8,128)(2,1)S(1)}, bf16[16,2,16,128]{3,2,1,0:T(8,128)(2,1)S(1)}, u32[]{:S(2)}, u32[]{:S(2)}) collective-permute-start(bf16[16,2,16,128]{3,2,1,0:T(8,128)(2,1)S(1)} %get-tuple-element.6), channel_id=1, source_target_pairs={{0,1},{1,2},{2,3},{3,0},{4,5},{5,6},{6,7},{7,4},{8,9},{9,10},{10,1... | collective-permute-start | bytes 393224 | tf_op jit(solution)/shard_map/ppermute | solution.py:229
  149.9 4.3 %collective-permute-start.2 = (bf16[16,2,16,128]{3,2,1,0:T(8,128)(2,1)S(1)}, bf16[16,2,16,128]{3,2,1,0:T(8,128)(2,1)S(1)}, u32[]{:S(2)}, u32[]{:S(2)}) collective-permute-start(bf16[16,2,16,128]{3,2,1,0:T(8,128)(2,1)S(1)} %get-tuple-element.6), channel_id=1, source_target_pairs={{0,3},{1,0},{2,1},{3,2},{4,7},{5,4},{6,5},{7,6},{8,11},{9,8},{10,9... | collective-permute-start | bytes 393224 | tf_op jit(solution)/shard_map/ppermute | solution.py:229
  154.2 0.0 collective-permute-done.1
  154.2 1.0 collective-permute-done
  155.2 1.0 collective-permute-done.2
  156.2 0.1 pad_maximum_fusion.own
  156.3 4.3 %collective-permute-start.3 = (bf16[4,16,2,16,128]{4,3,2,1,0:T(8,128)(2,1)S(1)}, bf16[4,16,2,16,128]{4,3,2,1,0:T(8,128)(2,1)S(1)}, u32[]{:S(2)}, u32[]{:S(2)}) collective-permute-start(bf16[4,16,2,16,128]{4,3,2,1,0:T(8,128)(2,1)S(1)} %pad_maximum_fusion.own), channel_id=1, source_target_pairs={{0,32},{32,0},{1,33},{33,1},{2,34},{34,2},{3,35},{35,3},{4,36},{36... | collective-permute-start | bytes 1572872 | tf_op jit(solution)/shard_map/ppermute | solution.py:231
  160.6 1.5 collective-permute-done.3.other
  162.2 0.0 all-to-all-done.5.state
  162.2 1.1 contract.3
  (2 shorter events, 0.1 us)
Async XLA Ops:
  0.0 25.4 %copy-start.1 = (s32[3]{0:T(128)S(1)}, s32[3]{0:T(128)}, u32[]{:S(2)}) copy-start(s32[3]{0:T(128)} %owners.5) | copy-start | bytes 40
  3.2 82.3 %copy-start = (bf16[2,512,128]{2,1,0:T(8,128)(2,1)S(1)}, bf16[2,512,128]{2,1,0:T(8,128)(2,1)}, u32[]{:S(2)}) copy-start(bf16[2,512,128]{2,1,0:T(8,128)(2,1)} %refs_0_.1) | copy-start | bytes 786436
  80.6 38.7 %all-to-all-start.3 = ((bf16[16,14,16,128]{3,2,1,0:T(8,128)(2,1)}), bf16[16,14,16,128]{3,2,1,0:T(8,128)(2,1)S(1)}, u32[]{:S(2)}, u32[]{:S(2)}) async-start(bf16[16,14,16,128]{3,2,1,0:T(8,128)(2,1)} %pack.1), calls=%async_computation.3 | async-start | bytes 1835008 | tf_op jit(solution)/shard_map/all_to_all | solution.py:206
  85.5 30.3 %collective-permute-start.6 = (bf16[2,512,128]{2,1,0:T(8,128)(2,1)S(1)}, bf16[2,512,128]{2,1,0:T(8,128)(2,1)S(1)}, u32[]{:S(2)}, u32[]{:S(2)}) collective-permute-start(bf16[2,512,128]{2,1,0:T(8,128)(2,1)S(1)} %copy-done), channel_id=1, source_target_pairs={{0,16},{16,0},{1,17},{17,1},{2,18},{18,2},{3,19},{19,3},{4,20},{20... | collective-permute-start | bytes 786440 | tf_op jit(solution)/shard_map/ppermute | solution.py:210
  87.7 30.4 %collective-permute-start.5 = (bf16[2,512,128]{2,1,0:T(8,128)(2,1)S(1)}, bf16[2,512,128]{2,1,0:T(8,128)(2,1)S(1)}, u32[]{:S(2)}, u32[]{:S(2)}) collective-permute-start(bf16[2,512,128]{2,1,0:T(8,128)(2,1)S(1)} %copy-done), channel_id=1, source_target_pairs={{0,32},{32,0},{1,33},{33,1},{2,34},{34,2},{3,35},{35,3},{4,36},{36... | collective-permute-start | bytes 786440 | tf_op jit(solution)/shard_map/ppermute | solution.py:211
  115.8 3.5 %collective-permute-start.7 = (bf16[2,512,128]{2,1,0:T(8,128)(2,1)S(1)}, bf16[2,512,128]{2,1,0:T(8,128)(2,1)S(1)}, u32[]{:S(2)}, u32[]{:S(2)}) collective-permute-start(bf16[2,512,128]{2,1,0:T(8,128)(2,1)S(1)} %collective-permute-done.6.refs_2_), channel_id=1, source_target_pairs={{0,32},{32,0},{1,33},{33,1},{2,34},{34,2},{3,35},{35,3},{4,36},{36... | collective-permute-start | bytes 786440 | tf_op jit(solution)/shard_map/ppermute | solution.py:212
  120.5 15.8 %all-to-all-start.4 = ((bf16[32,2,16,128]{3,2,1,0:T(8,128)(2,1)}), bf16[32,2,16,128]{3,2,1,0:T(8,128)(2,1)S(1)}, u32[]{:S(2)}, u32[]{:S(2)}) async-start(bf16[32,2,16,128]{3,2,1,0:T(8,128)(2,1)} %bitcast.4), calls=%async_computation.4 | async-start | bytes 524288 | tf_op jit(solution)/shard_map/all_to_all | solution.py:206
  125.5 3.8 %collective-permute-start.4 = (bf16[16,8,16,128]{3,2,1,0:T(8,128)(2,1)S(1)}, bf16[16,8,16,128]{3,2,1,0:T(8,128)(2,1)S(1)}, u32[]{:S(2)}, u32[]{:S(2)}) collective-permute-start(bf16[16,8,16,128]{3,2,1,0:T(8,128)(2,1)S(1)} %slice.9.own), channel_id=1, source_target_pairs={{0,32},{32,0},{1,33},{33,1},{2,34},{34,2},{3,35},{35,3},{4,36},{36... | collective-permute-start | bytes 1572872 | tf_op jit(solution)/shard_map/ppermute | solution.py:224
  137.4 24.8 %all-to-all-start.5 = ((bf16[32,2,16,128]{3,2,1,0:T(8,128)(2,1)}), bf16[32,2,16,128]{3,2,1,0:T(8,128)(2,1)S(1)}, u32[]{:S(2)}, u32[]{:S(2)}) async-start(bf16[32,2,16,128]{3,2,1,0:T(8,128)(2,1)} %contract.2), calls=%async_computation.5 | async-start | bytes 524288 | tf_op jit(solution)/shard_map/all_to_all | solution.py:206
  143.1 11.2 %collective-permute-start.1 = (bf16[16,2,16,128]{3,2,1,0:T(8,128)(2,1)S(1)}, bf16[16,2,16,128]{3,2,1,0:T(8,128)(2,1)S(1)}, u32[]{:S(2)}, u32[]{:S(2)}) collective-permute-start(bf16[16,2,16,128]{3,2,1,0:T(8,128)(2,1)S(1)} %get-tuple-element.6), channel_id=1, source_target_pairs={{0,2},{1,3},{2,0},{3,1},{4,6},{5,7},{6,4},{7,5},{8,10},{9,11},{10,... | collective-permute-start | bytes 393224 | tf_op jit(solution)/shard_map/ppermute | solution.py:229
  147.7 7.5 %collective-permute-start = (bf16[16,2,16,128]{3,2,1,0:T(8,128)(2,1)S(1)}, bf16[16,2,16,128]{3,2,1,0:T(8,128)(2,1)S(1)}, u32[]{:S(2)}, u32[]{:S(2)}) collective-permute-start(bf16[16,2,16,128]{3,2,1,0:T(8,128)(2,1)S(1)} %get-tuple-element.6), channel_id=1, source_target_pairs={{0,1},{1,2},{2,3},{3,0},{4,5},{5,6},{6,7},{7,4},{8,9},{9,10},{10,1... | collective-permute-start | bytes 393224 | tf_op jit(solution)/shard_map/ppermute | solution.py:229
  149.9 6.3 %collective-permute-start.2 = (bf16[16,2,16,128]{3,2,1,0:T(8,128)(2,1)S(1)}, bf16[16,2,16,128]{3,2,1,0:T(8,128)(2,1)S(1)}, u32[]{:S(2)}, u32[]{:S(2)}) collective-permute-start(bf16[16,2,16,128]{3,2,1,0:T(8,128)(2,1)S(1)} %get-tuple-element.6), channel_id=1, source_target_pairs={{0,3},{1,0},{2,1},{3,2},{4,7},{5,4},{6,5},{7,6},{8,11},{9,8},{10,9... | collective-permute-start | bytes 393224 | tf_op jit(solution)/shard_map/ppermute | solution.py:229
  156.3 5.9 %collective-permute-start.3 = (bf16[4,16,2,16,128]{4,3,2,1,0:T(8,128)(2,1)S(1)}, bf16[4,16,2,16,128]{4,3,2,1,0:T(8,128)(2,1)S(1)}, u32[]{:S(2)}, u32[]{:S(2)}) collective-permute-start(bf16[4,16,2,16,128]{4,3,2,1,0:T(8,128)(2,1)S(1)} %pad_maximum_fusion.own), channel_id=1, source_target_pairs={{0,32},{32,0},{1,33},{33,1},{2,34},{34,2},{3,35},{35,3},{4,36},{36... | collective-permute-start | bytes 1572872 | tf_op jit(solution)/shard_map/ppermute | solution.py:231

commit v5 on v4

--- a/solution.py
+++ b/solution.py
@@ -21,24 +21,23 @@
     return (lax.axis_index("x") * 4 + lax.axis_index("zh")) * 2 + lax.axis_index("core")
 
 
-def slice_kernel(owners, slices, relabels, left, right, out, l_own, r_own, sems):
+def slice_kernel(owners_in, slices_in, relabels_in, left, right, out, owners, slices, relabels, l_own, r_own, sems):
+    at_z, at_y = lax.axis_index("za") * 4 + lax.axis_index("zb"), lax.axis_index("y")
+    blocks = (at_z * 4 + at_y, at_y * 8 + at_z, (at_z >> 1) * 8 + at_y * 2 + (at_z & 1))
+    pairs = [(owners_in, owners), (slices_in, slices), (relabels_in, relabels)]
+    pairs += [(left.at[0, :, pl.ds(pl.multiple_of(block * 16, 16), 16)], l_own.at[k]) for k, block in enumerate(blocks)]
+    pairs += [(right.at[0, s], r_own.at[s]) for s in range(2)]
+    copies = [pltpu.make_async_copy(source, target, sems.at[i]) for i, (source, target) in enumerate(pairs)]
+    for copy in copies:
+        copy.start()
+    for copy in copies[:3]:
+        copy.wait()
     row = own_row()
     used = [owners[k] == row for k in range(3)]
-    chosen = jnp.int32(0)
+    chosen, place_in_order = jnp.int32(0), jnp.int32(0)
     for k in range(3):
         chosen = jnp.where(used[k], slices[k], chosen)
-    at_z, at_y = lax.axis_index("za") * 4 + lax.axis_index("zb"), lax.axis_index("y")
-    block = jnp.where(used[0], at_z * 4 + at_y, at_y * 8 + at_z)
-    block = jnp.where(used[2], (at_z >> 1) * 8 + at_y * 2 + (at_z & 1), block)
-    rows = pl.ds(pl.multiple_of(block * 16, 16), 16)
-    copies = [
-        pltpu.make_async_copy(right.at[0, chosen, 0], r_own.at[0], sems.at[0]),
-        pltpu.make_async_copy(right.at[0, chosen, 1], r_own.at[1], sems.at[1]),
-        pltpu.make_async_copy(left.at[0, 0, rows], l_own.at[0], sems.at[2]),
-        pltpu.make_async_copy(left.at[0, 1, rows], l_own.at[1], sems.at[3]),
-    ]
-    for copy in copies:
-        copy.start()
+        place_in_order = jnp.where(used[k], k, place_in_order)
     q = lax.broadcasted_iota(jnp.int32, (512, 512), 0)
     arrived = (((q >> 3) & 1) << 8) | (((q >> 4) & 15) << 4) | (((q >> 8) & 1) << 3) | (q & 7)
     place = jnp.where(used[1], arrived, q)
@@ -46,11 +45,11 @@
     mapping = jnp.where(used[1], relabels[0:1, :], mapping)
     mapping = jnp.where(used[2], relabels[1:2, :], mapping)
     onehot = jnp.where(place == mapping, 1.0, 0.0).astype(BF16)
-    for copy in copies:
+    for copy in copies[3:]:
         copy.wait()
-    both = jnp.concatenate([l_own[0], l_own[1]], axis=0)
-    by_real = jnp.dot(both, r_own[0], preferred_element_type=F32)
-    by_imag = jnp.dot(both, r_own[1], preferred_element_type=F32)
+    both = jnp.concatenate([l_own[place_in_order, 0], l_own[place_in_order, 1]], axis=0)
+    by_real = jnp.dot(both, r_own[chosen, 0], preferred_element_type=F32)
+    by_imag = jnp.dot(both, r_own[chosen, 1], preferred_element_type=F32)
     real = by_real[:16] - by_imag[16:]
     imag = by_imag[:16] + by_real[16:]
     branch = jnp.concatenate([real, imag], axis=0).astype(BF16)
@@ -71,12 +70,15 @@
 def branch_slice(owners, slices, relabels, left, right):
     return pl.pallas_call(
         slice_kernel,
-        in_specs=[SMEM, SMEM, VMEM, HBM, HBM],
+        in_specs=[HBM] * 5,
         out_specs=VMEM,
         scratch_shapes=[
-            pltpu.VMEM((2, 16, 512), BF16),
-            pltpu.VMEM((2, 512, 512), BF16),
-            pltpu.SemaphoreType.DMA((4,)),
+            pltpu.SMEM((3,), jnp.int32),
+            pltpu.SMEM((3,), jnp.int32),
+            pltpu.VMEM((2, 512), jnp.int32),
+            pltpu.VMEM((3, 2, 16, 512), BF16),
+            pltpu.VMEM((2, 2, 512, 512), BF16),
+            pltpu.SemaphoreType.DMA((8,)),
         ],
         out_shape=jax.ShapeDtypeStruct((8, *TILE), BF16),
         name="branch_slice",

time: 164 us -> 164 us (level)
  no operation moved by 1% of the time
where the time goes in v5:
time: 164 us; the launch traced here: 163 us
  blocking collectives  75.2 us (46%)
  starting transfers between devices  43 us (26%)
  waiting for transfers between devices  36.3 us (22%)
  Pallas kernels  8.39 us (5%)
    all_to_all x3, blocking collectives, send(): return lax.all_to_all(blocks, axes, 0, 0, tiled=True)  75.2 us
    ppermute x1, waiting for transfers between devices, steps(): across = lax.ppermute(stem, 'za', FLIP)  23 us
    all_to_all x3, starting transfers between devices, send(): return lax.all_to_all(blocks, axes, 0, 0, tiled=True)  15.7 us
    ppermute x3, starting transfers between devices, steps(): lax.ppermute(last, 'y', [(i, (i + offset) % 4) for i in range(4)])  11.1 us
    all_to_all x3, waiting for transfers between devices, send(): return lax.all_to_all(blocks, axes, 0, 0, tiled=True)  6.96 us
    ppermute x1, starting transfers between devices, steps(): beside = lax.ppermute(stem, 'core', FLIP)  5.06 us
    ppermute x1, starting transfers between devices, steps(): other = lax.ppermute(last, 'core', FLIP)  4.34 us
  transfers between devices with their start and end apart: 11, of which 7 were waited for; matrix products, arithmetic and copies ran while one was open for 0% of the time, Pallas kernels for 0%

profile of v5, /device:TPU:1, one launch (start us, length us, event | category | flops | bytes accessed | tf_op | source)
XLA Modules:
  0.0 163.2 jit_solution(6468943397580577198)
XLA Ops:
  0.0 0.0 copy-start.1
  0.0 2.8 %branch_slice.1 = bf16[8,16,128]{2,1,0:T(8,128)(2,1)} custom-call(s32[3]{0:T(128)} %owners.3, s32[3]{0:T(128)} %slices_in.1, s32[2,512]{1,0:T(2,128)} %relabels_in.1, bf16[1,2,512,512]{3,2,1,0:T(8,128)(2,1)} %left.1, bf16[1,2,2,512,512]{4,3,2,1,0:T(8,128)(2,1)} %right.1), custom_call_target="tpu_custom_call" | custom-call | tf_op jit(solution)/shard_map/branch_slice/pallas_call | solution.py:71
  2.8 0.0 copy-start
  2.8 22.2 %all_to_all.30.tiles = bf16[8,16,128]{2,1,0:T(8,128)(2,1)S(1)} all-to-all(bf16[8,16,128]{2,1,0:T(8,128)(2,1)} %branch_slice.1), channel_id=1, replica_groups=mesh['x'=4,'zh'=4,'core'=2,'za'=2,'zb'=4,'y'=4] {'x','core'}, dimensions={0} | all-to-all | bytes 65536 | tf_op jit(solution)/shard_map/all_to_all | solution.py:208
  25.0 0.0 copy-done.1
  25.0 0.6 pick.2
  25.6 38.2 %all_to_all.31.tiles = bf16[4,3,16,128]{3,2,1,0:T(8,128)(2,1)S(1)} all-to-all(bf16[4,3,16,128]{3,2,1,0:T(8,128)(2,1)S(1)} %pick.2), channel_id=1, replica_groups=mesh['x'=4,'zh'=4,'core'=2,'za'=2,'zb'=4,'y'=4] {'zh'}, dimensions={0} | all-to-all | bytes 98304 | tf_op jit(solution)/shard_map/all_to_all | solution.py:208
  63.8 0.6 pick.3
  64.3 14.9 %all_to_all.32.tiles = bf16[8,3,16,128]{3,2,1,0:T(8,128)(2,1)S(1)} all-to-all(bf16[8,3,16,128]{3,2,1,0:T(8,128)(2,1)S(1)} %pick.3), channel_id=1, replica_groups=mesh['x'=4,'zh'=4,'core'=2,'za'=2,'zb'=4,'y'=4] {'za','zb'}, dimensions={0} | all-to-all | bytes 196608 | tf_op jit(solution)/shard_map/all_to_all | solution.py:208
  79.2 1.0 pack.1
  80.2 5.0 %all-to-all-start.3 = ((bf16[16,14,16,128]{3,2,1,0:T(8,128)(2,1)}), bf16[16,14,16,128]{3,2,1,0:T(8,128)(2,1)S(1)}, u32[]{:S(2)}, u32[]{:S(2)}) async-start(bf16[16,14,16,128]{3,2,1,0:T(8,128)(2,1)} %pack.1), calls=%async_computation.3 | async-start | bytes 1835008 | tf_op jit(solution)/shard_map/all_to_all | solution.py:208
  85.2 0.0 copy-done
  85.2 2.2 %collective-permute-start.6 = (bf16[2,512,128]{2,1,0:T(8,128)(2,1)S(1)}, bf16[2,512,128]{2,1,0:T(8,128)(2,1)S(1)}, u32[]{:S(2)}, u32[]{:S(2)}) collective-permute-start(bf16[2,512,128]{2,1,0:T(8,128)(2,1)S(1)} %copy-done), channel_id=1, source_target_pairs={{0,16},{16,0},{1,17},{17,1},{2,18},{18,2},{3,19},{19,3},{4,20},{20... | collective-permute-start | bytes 786440 | tf_op jit(solution)/shard_map/ppermute | solution.py:212
  87.4 5.1 %collective-permute-start.5 = (bf16[2,512,128]{2,1,0:T(8,128)(2,1)S(1)}, bf16[2,512,128]{2,1,0:T(8,128)(2,1)S(1)}, u32[]{:S(2)}, u32[]{:S(2)}) collective-permute-start(bf16[2,512,128]{2,1,0:T(8,128)(2,1)S(1)} %copy-done), channel_id=1, source_target_pairs={{0,32},{32,0},{1,33},{33,1},{2,34},{34,2},{3,35},{35,3},{4,36},{36... | collective-permute-start | bytes 786440 | tf_op jit(solution)/shard_map/ppermute | solution.py:213
  92.5 23.0 %collective-permute-done.6.refs_2_ = bf16[2,512,128]{2,1,0:T(8,128)(2,1)S(1)} collective-permute-done((bf16[2,512,128]{2,1,0:T(8,128)(2,1)S(1)}, bf16[2,512,128]{2,1,0:T(8,128)(2,1)S(1)}, u32[]{:S(2)}, u32[]{:S(2)}) %collective-permute-start.6) | collective-permute-done | bytes 262176 | tf_op jit(solution)/shard_map/ppermute | solution.py:212
  115.5 2.4 %collective-permute-start.7 = (bf16[2,512,128]{2,1,0:T(8,128)(2,1)S(1)}, bf16[2,512,128]{2,1,0:T(8,128)(2,1)S(1)}, u32[]{:S(2)}, u32[]{:S(2)}) collective-permute-start(bf16[2,512,128]{2,1,0:T(8,128)(2,1)S(1)} %collective-permute-done.6.refs_2_), channel_id=1, source_target_pairs={{0,32},{32,0},{1,33},{33,1},{2,34},{34,2},{3,35},{35,3},{4,36},{36... | collective-permute-start | bytes 786440 | tf_op jit(solution)/shard_map/ppermute | solution.py:214
  117.9 0.0 collective-permute-done.5.refs_1_
  117.9 1.1 collective-permute-done.7.refs_3_
  119.0 0.0 all-to-all-done.3.held
  119.0 1.2 first_contract.1
  120.2 5.0 %all-to-all-start.4 = ((bf16[32,2,16,128]{3,2,1,0:T(8,128)(2,1)}), bf16[32,2,16,128]{3,2,1,0:T(8,128)(2,1)S(1)}, u32[]{:S(2)}, u32[]{:S(2)}) async-start(bf16[32,2,16,128]{3,2,1,0:T(8,128)(2,1)} %bitcast.4), calls=%async_computation.4 | async-start | bytes 524288 | tf_op jit(solution)/shard_map/all_to_all | solution.py:208
  125.2 2.1 %collective-permute-start.4 = (bf16[16,8,16,128]{3,2,1,0:T(8,128)(2,1)S(1)}, bf16[16,8,16,128]{3,2,1,0:T(8,128)(2,1)S(1)}, u32[]{:S(2)}, u32[]{:S(2)}) collective-permute-start(bf16[16,8,16,128]{3,2,1,0:T(8,128)(2,1)S(1)} %slice.9.own), channel_id=1, source_target_pairs={{0,32},{32,0},{1,33},{33,1},{2,34},{34,2},{3,35},{35,3},{4,36},{36... | collective-permute-start | bytes 1572872 | tf_op jit(solution)/shard_map/ppermute | solution.py:226
  127.3 1.7 %collective-permute-done.4.other = bf16[16,8,16,128]{3,2,1,0:T(8,128)(2,1)S(1)} collective-permute-done((bf16[16,8,16,128]{3,2,1,0:T(8,128)(2,1)S(1)}, bf16[16,8,16,128]{3,2,1,0:T(8,128)(2,1)S(1)}, u32[]{:S(2)}, u32[]{:S(2)}) %collective-permute-start.4) | collective-permute-done | bytes 524320 | tf_op jit(solution)/shard_map/ppermute | solution.py:226
  129.0 7.0 %all-to-all-done.4.state = bf16[32,2,16,128]{3,2,1,0:T(8,128)(2,1)S(1)} async-done(((bf16[32,2,16,128]{3,2,1,0:T(8,128)(2,1)}), bf16[32,2,16,128]{3,2,1,0:T(8,128)(2,1)S(1)}, u32[]{:S(2)}, u32[]{:S(2)}) %all-to-all-start.4) | async-done | bytes 262176 | tf_op jit(solution)/shard_map/all_to_all | solution.py:208
  135.9 1.1 contract.2
  137.1 5.8 %all-to-all-start.5 = ((bf16[32,2,16,128]{3,2,1,0:T(8,128)(2,1)}), bf16[32,2,16,128]{3,2,1,0:T(8,128)(2,1)S(1)}, u32[]{:S(2)}, u32[]{:S(2)}) async-start(bf16[32,2,16,128]{3,2,1,0:T(8,128)(2,1)} %contract.2), calls=%async_computation.5 | async-start | bytes 524288 | tf_op jit(solution)/shard_map/all_to_all | solution.py:208
  143.0 4.6 %collective-permute-start.1 = (bf16[16,2,16,128]{3,2,1,0:T(8,128)(2,1)S(1)}, bf16[16,2,16,128]{3,2,1,0:T(8,128)(2,1)S(1)}, u32[]{:S(2)}, u32[]{:S(2)}) collective-permute-start(bf16[16,2,16,128]{3,2,1,0:T(8,128)(2,1)S(1)} %get-tuple-element.6), channel_id=1, source_target_pairs={{0,2},{1,3},{2,0},{3,1},{4,6},{5,7},{6,4},{7,5},{8,10},{9,11},{10,... | collective-permute-start | bytes 393224 | tf_op jit(solution)/shard_map/ppermute | solution.py:231
  147.6 2.2 %collective-permute-start = (bf16[16,2,16,128]{3,2,1,0:T(8,128)(2,1)S(1)}, bf16[16,2,16,128]{3,2,1,0:T(8,128)(2,1)S(1)}, u32[]{:S(2)}, u32[]{:S(2)}) collective-permute-start(bf16[16,2,16,128]{3,2,1,0:T(8,128)(2,1)S(1)} %get-tuple-element.6), channel_id=1, source_target_pairs={{0,1},{1,2},{2,3},{3,0},{4,5},{5,6},{6,7},{7,4},{8,9},{9,10},{10,1... | collective-permute-start | bytes 393224 | tf_op jit(solution)/shard_map/ppermute | solution.py:231
  149.8 4.3 %collective-permute-start.2 = (bf16[16,2,16,128]{3,2,1,0:T(8,128)(2,1)S(1)}, bf16[16,2,16,128]{3,2,1,0:T(8,128)(2,1)S(1)}, u32[]{:S(2)}, u32[]{:S(2)}) collective-permute-start(bf16[16,2,16,128]{3,2,1,0:T(8,128)(2,1)S(1)} %get-tuple-element.6), channel_id=1, source_target_pairs={{0,3},{1,0},{2,1},{3,2},{4,7},{5,4},{6,5},{7,6},{8,11},{9,8},{10,9... | collective-permute-start | bytes 393224 | tf_op jit(solution)/shard_map/ppermute | solution.py:231
  154.1 0.0 collective-permute-done.1
  154.1 1.0 collective-permute-done
  155.1 1.0 collective-permute-done.2
  156.1 0.1 pad_maximum_fusion.own
  156.2 4.3 %collective-permute-start.3 = (bf16[4,16,2,16,128]{4,3,2,1,0:T(8,128)(2,1)S(1)}, bf16[4,16,2,16,128]{4,3,2,1,0:T(8,128)(2,1)S(1)}, u32[]{:S(2)}, u32[]{:S(2)}) collective-permute-start(bf16[4,16,2,16,128]{4,3,2,1,0:T(8,128)(2,1)S(1)} %pad_maximum_fusion.own), channel_id=1, source_target_pairs={{0,32},{32,0},{1,33},{33,1},{2,34},{34,2},{3,35},{35,3},{4,36},{36... | collective-permute-start | bytes 1572872 | tf_op jit(solution)/shard_map/ppermute | solution.py:233
  160.5 1.5 collective-permute-done.3.other
  162.0 0.0 all-to-all-done.5.state
  162.0 1.1 contract.3
  (2 shorter events, 0.1 us)
Async XLA Ops:
  0.0 25.0 %copy-start.1 = (s32[3]{0:T(128)S(1)}, s32[3]{0:T(128)}, u32[]{:S(2)}) copy-start(s32[3]{0:T(128)} %owners.3) | copy-start | bytes 40
  2.8 82.4 %copy-start = (bf16[2,512,128]{2,1,0:T(8,128)(2,1)S(1)}, bf16[2,512,128]{2,1,0:T(8,128)(2,1)}, u32[]{:S(2)}) copy-start(bf16[2,512,128]{2,1,0:T(8,128)(2,1)} %refs_0_.1) | copy-start | bytes 786436
  80.2 38.8 %all-to-all-start.3 = ((bf16[16,14,16,128]{3,2,1,0:T(8,128)(2,1)}), bf16[16,14,16,128]{3,2,1,0:T(8,128)(2,1)S(1)}, u32[]{:S(2)}, u32[]{:S(2)}) async-start(bf16[16,14,16,128]{3,2,1,0:T(8,128)(2,1)} %pack.1), calls=%async_computation.3 | async-start | bytes 1835008 | tf_op jit(solution)/shard_map/all_to_all | solution.py:208
  85.2 30.3 %collective-permute-start.6 = (bf16[2,512,128]{2,1,0:T(8,128)(2,1)S(1)}, bf16[2,512,128]{2,1,0:T(8,128)(2,1)S(1)}, u32[]{:S(2)}, u32[]{:S(2)}) collective-permute-start(bf16[2,512,128]{2,1,0:T(8,128)(2,1)S(1)} %copy-done), channel_id=1, source_target_pairs={{0,16},{16,0},{1,17},{17,1},{2,18},{18,2},{3,19},{19,3},{4,20},{20... | collective-permute-start | bytes 786440 | tf_op jit(solution)/shard_map/ppermute | solution.py:212
  87.4 30.5 %collective-permute-start.5 = (bf16[2,512,128]{2,1,0:T(8,128)(2,1)S(1)}, bf16[2,512,128]{2,1,0:T(8,128)(2,1)S(1)}, u32[]{:S(2)}, u32[]{:S(2)}) collective-permute-start(bf16[2,512,128]{2,1,0:T(8,128)(2,1)S(1)} %copy-done), channel_id=1, source_target_pairs={{0,32},{32,0},{1,33},{33,1},{2,34},{34,2},{3,35},{35,3},{4,36},{36... | collective-permute-start | bytes 786440 | tf_op jit(solution)/shard_map/ppermute | solution.py:213
  115.5 3.5 %collective-permute-start.7 = (bf16[2,512,128]{2,1,0:T(8,128)(2,1)S(1)}, bf16[2,512,128]{2,1,0:T(8,128)(2,1)S(1)}, u32[]{:S(2)}, u32[]{:S(2)}) collective-permute-start(bf16[2,512,128]{2,1,0:T(8,128)(2,1)S(1)} %collective-permute-done.6.refs_2_), channel_id=1, source_target_pairs={{0,32},{32,0},{1,33},{33,1},{2,34},{34,2},{3,35},{35,3},{4,36},{36... | collective-permute-start | bytes 786440 | tf_op jit(solution)/shard_map/ppermute | solution.py:214
  120.2 15.8 %all-to-all-start.4 = ((bf16[32,2,16,128]{3,2,1,0:T(8,128)(2,1)}), bf16[32,2,16,128]{3,2,1,0:T(8,128)(2,1)S(1)}, u32[]{:S(2)}, u32[]{:S(2)}) async-start(bf16[32,2,16,128]{3,2,1,0:T(8,128)(2,1)} %bitcast.4), calls=%async_computation.4 | async-start | bytes 524288 | tf_op jit(solution)/shard_map/all_to_all | solution.py:208
  125.2 3.8 %collective-permute-start.4 = (bf16[16,8,16,128]{3,2,1,0:T(8,128)(2,1)S(1)}, bf16[16,8,16,128]{3,2,1,0:T(8,128)(2,1)S(1)}, u32[]{:S(2)}, u32[]{:S(2)}) collective-permute-start(bf16[16,8,16,128]{3,2,1,0:T(8,128)(2,1)S(1)} %slice.9.own), channel_id=1, source_target_pairs={{0,32},{32,0},{1,33},{33,1},{2,34},{34,2},{3,35},{35,3},{4,36},{36... | collective-permute-start | bytes 1572872 | tf_op jit(solution)/shard_map/ppermute | solution.py:226
  137.1 25.0 %all-to-all-start.5 = ((bf16[32,2,16,128]{3,2,1,0:T(8,128)(2,1)}), bf16[32,2,16,128]{3,2,1,0:T(8,128)(2,1)S(1)}, u32[]{:S(2)}, u32[]{:S(2)}) async-start(bf16[32,2,16,128]{3,2,1,0:T(8,128)(2,1)} %contract.2), calls=%async_computation.5 | async-start | bytes 524288 | tf_op jit(solution)/shard_map/all_to_all | solution.py:208
  143.0 11.2 %collective-permute-start.1 = (bf16[16,2,16,128]{3,2,1,0:T(8,128)(2,1)S(1)}, bf16[16,2,16,128]{3,2,1,0:T(8,128)(2,1)S(1)}, u32[]{:S(2)}, u32[]{:S(2)}) collective-permute-start(bf16[16,2,16,128]{3,2,1,0:T(8,128)(2,1)S(1)} %get-tuple-element.6), channel_id=1, source_target_pairs={{0,2},{1,3},{2,0},{3,1},{4,6},{5,7},{6,4},{7,5},{8,10},{9,11},{10,... | collective-permute-start | bytes 393224 | tf_op jit(solution)/shard_map/ppermute | solution.py:231
  147.6 7.5 %collective-permute-start = (bf16[16,2,16,128]{3,2,1,0:T(8,128)(2,1)S(1)}, bf16[16,2,16,128]{3,2,1,0:T(8,128)(2,1)S(1)}, u32[]{:S(2)}, u32[]{:S(2)}) collective-permute-start(bf16[16,2,16,128]{3,2,1,0:T(8,128)(2,1)S(1)} %get-tuple-element.6), channel_id=1, source_target_pairs={{0,1},{1,2},{2,3},{3,0},{4,5},{5,6},{6,7},{7,4},{8,9},{9,10},{10,1... | collective-permute-start | bytes 393224 | tf_op jit(solution)/shard_map/ppermute | solution.py:231
  149.8 6.3 %collective-permute-start.2 = (bf16[16,2,16,128]{3,2,1,0:T(8,128)(2,1)S(1)}, bf16[16,2,16,128]{3,2,1,0:T(8,128)(2,1)S(1)}, u32[]{:S(2)}, u32[]{:S(2)}) collective-permute-start(bf16[16,2,16,128]{3,2,1,0:T(8,128)(2,1)S(1)} %get-tuple-element.6), channel_id=1, source_target_pairs={{0,3},{1,0},{2,1},{3,2},{4,7},{5,4},{6,5},{7,6},{8,11},{9,8},{10,9... | collective-permute-start | bytes 393224 | tf_op jit(solution)/shard_map/ppermute | solution.py:231
  156.2 5.9 %collective-permute-start.3 = (bf16[4,16,2,16,128]{4,3,2,1,0:T(8,128)(2,1)S(1)}, bf16[4,16,2,16,128]{4,3,2,1,0:T(8,128)(2,1)S(1)}, u32[]{:S(2)}, u32[]{:S(2)}) collective-permute-start(bf16[4,16,2,16,128]{4,3,2,1,0:T(8,128)(2,1)S(1)} %pad_maximum_fusion.own), channel_id=1, source_target_pairs={{0,32},{32,0},{1,33},{33,1},{2,34},{34,2},{3,35},{35,3},{4,36},{36... | collective-permute-start | bytes 1572872 | tf_op jit(solution)/shard_map/ppermute | solution.py:233

commit v6 on v5

--- a/solution.py
+++ b/solution.py
@@ -26,7 +26,8 @@
     blocks = (at_z * 4 + at_y, at_y * 8 + at_z, (at_z >> 1) * 8 + at_y * 2 + (at_z & 1))
     pairs = [(owners_in, owners), (slices_in, slices), (relabels_in, relabels)]
     pairs += [(left.at[0, :, pl.ds(pl.multiple_of(block * 16, 16), 16)], l_own.at[k]) for k, block in enumerate(blocks)]
-    pairs += [(right.at[0, s], r_own.at[s]) for s in range(2)]
+    depths = [pl.ds(i * 128, 128) for i in range(4)]
+    pairs += [(right.at[0, s, :, depth], r_own.at[s, :, depth]) for depth in depths for s in range(2)]
     copies = [pltpu.make_async_copy(source, target, sems.at[i]) for i, (source, target) in enumerate(pairs)]
     for copy in copies:
         copy.start()
@@ -45,11 +46,16 @@
     mapping = jnp.where(used[1], relabels[0:1, :], mapping)
     mapping = jnp.where(used[2], relabels[1:2, :], mapping)
     onehot = jnp.where(place == mapping, 1.0, 0.0).astype(BF16)
-    for copy in copies[3:]:
+    for copy in copies[3:6]:
         copy.wait()
     both = jnp.concatenate([l_own[place_in_order, 0], l_own[place_in_order, 1]], axis=0)
-    by_real = jnp.dot(both, r_own[chosen, 0], preferred_element_type=F32)
-    by_imag = jnp.dot(both, r_own[chosen, 1], preferred_element_type=F32)
+    by_real, by_imag = jnp.zeros((32, 512), F32), jnp.zeros((32, 512), F32)
+    for i, depth in enumerate(depths):
+        for copy in copies[6 + 2 * i : 8 + 2 * i]:
+            copy.wait()
+        some = both[:, i * 128 : i * 128 + 128]
+        by_real += jnp.dot(some, r_own[chosen, 0, depth], preferred_element_type=F32)
+        by_imag += jnp.dot(some, r_own[chosen, 1, depth], preferred_element_type=F32)
     real = by_real[:16] - by_imag[16:]
     imag = by_imag[:16] + by_real[16:]
     branch = jnp.concatenate([real, imag], axis=0).astype(BF16)
@@ -78,7 +84,7 @@
             pltpu.VMEM((2, 512), jnp.int32),
             pltpu.VMEM((3, 2, 16, 512), BF16),
             pltpu.VMEM((2, 2, 512, 512), BF16),
-            pltpu.SemaphoreType.DMA((8,)),
+            pltpu.SemaphoreType.DMA((14,)),
         ],
         out_shape=jax.ShapeDtypeStruct((8, *TILE), BF16),
         name="branch_slice",
@@ -104,23 +110,27 @@
     )(owners, tiles)
 
 
-def pack_kernel(tiles, out):
+def pack_kernel(tiles, out, block, sems):
     half = lax.axis_index("za") * 4
     for j in range(12):
         tile = tiles[half + j, 0] if j < 4 else tiles[j - 4, 1]
-        for i in range(16):
-            out[i, j] = tile
+        for y in range(4):
+            block[y, j] = tile
     for j in range(8):
-        tile = tiles[j, 2]
-        for x in range(4):
-            out[x * 4 + j // 2, 12 + j % 2] = tile
+        block[j // 2, 12 + j % 2] = tiles[j, 2]
+    copies = [pltpu.make_async_copy(block, out.at[pl.ds(x * 4, 4)], sems.at[x]) for x in range(4)]
+    for copy in copies:
+        copy.start()
+    for copy in copies:
+        copy.wait()
 
 
 def pack(tiles):
     return pl.pallas_call(
         pack_kernel,
         in_specs=[VMEM],
-        out_specs=VMEM,
+        out_specs=HBM,
+        scratch_shapes=[pltpu.VMEM((4, 14, *TILE), BF16), pltpu.SemaphoreType.DMA((4,))],
         out_shape=jax.ShapeDtypeStruct((16, 14, *TILE), BF16),
         compiler_params=SMALL,
         name="pack",

time: 164 us -> 164 us (level)
  no operation moved by 1% of the time
where the time goes in v6:
time: 164 us; the launch traced here: 163 us
  blocking collectives  75.3 us (46%)
  starting transfers between devices  42.8 us (26%)
  waiting for transfers between devices  36.2 us (22%)
  Pallas kernels  8.23 us (5%)
    all_to_all x3, blocking collectives, send(): return lax.all_to_all(blocks, axes, 0, 0, tiled=True)  75.3 us
    ppermute x1, waiting for transfers between devices, steps(): across = lax.ppermute(stem, 'za', FLIP)  22.9 us
    all_to_all x3, starting transfers between devices, send(): return lax.all_to_all(blocks, axes, 0, 0, tiled=True)  15.4 us
    ppermute x3, starting transfers between devices, steps(): lax.ppermute(last, 'y', [(i, (i + offset) % 4) for i in range(4)])  11.1 us
    all_to_all x3, waiting for transfers between devices, send(): return lax.all_to_all(blocks, axes, 0, 0, tiled=True)  6.96 us
    ppermute x1, starting transfers between devices, steps(): beside = lax.ppermute(stem, 'core', FLIP)  5.07 us
    ppermute x1, starting transfers between devices, steps(): other = lax.ppermute(last, 'core', FLIP)  4.34 us
  transfers between devices with their start and end apart: 11, of which 7 were waited for; matrix products, arithmetic and copies ran while one was open for 0% of the time, Pallas kernels for 0%

profile of v6, /device:TPU:1, one launch (start us, length us, event | category | flops | bytes accessed | tf_op | source)
XLA Modules:
  0.0 162.8 jit_solution(13256419571273751442)
XLA Ops:
  0.0 0.0 copy-start.1
  0.0 2.7 %branch_slice.1 = bf16[8,16,128]{2,1,0:T(8,128)(2,1)} custom-call(s32[3]{0:T(128)} %owners.3, s32[3]{0:T(128)} %slices_in.1, s32[2,512]{1,0:T(2,128)} %relabels_in.1, bf16[1,2,512,512]{3,2,1,0:T(8,128)(2,1)} %left.1, bf16[1,2,2,512,512]{4,3,2,1,0:T(8,128)(2,1)} %right.1), custom_call_target="tpu_custom_call" | custom-call | tf_op jit(solution)/shard_map/branch_slice/pallas_call | solution.py:77
  2.7 0.0 copy-start
  2.7 22.2 %all_to_all.30.tiles = bf16[8,16,128]{2,1,0:T(8,128)(2,1)S(1)} all-to-all(bf16[8,16,128]{2,1,0:T(8,128)(2,1)} %branch_slice.1), channel_id=1, replica_groups=mesh['x'=4,'zh'=4,'core'=2,'za'=2,'zb'=4,'y'=4] {'x','core'}, dimensions={0} | all-to-all | bytes 65536 | tf_op jit(solution)/shard_map/all_to_all | solution.py:218
  24.9 0.0 copy-done.1
  24.9 0.6 pick.2
  25.5 38.2 %all_to_all.31.tiles = bf16[4,3,16,128]{3,2,1,0:T(8,128)(2,1)S(1)} all-to-all(bf16[4,3,16,128]{3,2,1,0:T(8,128)(2,1)S(1)} %pick.2), channel_id=1, replica_groups=mesh['x'=4,'zh'=4,'core'=2,'za'=2,'zb'=4,'y'=4] {'zh'}, dimensions={0} | all-to-all | bytes 98304 | tf_op jit(solution)/shard_map/all_to_all | solution.py:218
  63.6 0.6 pick.3
  64.2 14.9 %all_to_all.32.tiles = bf16[8,3,16,128]{3,2,1,0:T(8,128)(2,1)S(1)} all-to-all(bf16[8,3,16,128]{3,2,1,0:T(8,128)(2,1)S(1)} %pick.3), channel_id=1, replica_groups=mesh['x'=4,'zh'=4,'core'=2,'za'=2,'zb'=4,'y'=4] {'za','zb'}, dimensions={0} | all-to-all | bytes 196608 | tf_op jit(solution)/shard_map/all_to_all | solution.py:218
  79.1 1.0 pack.1
  80.1 4.8 %all-to-all-start.3 = ((bf16[16,14,16,128]{3,2,1,0:T(8,128)(2,1)}), bf16[16,14,16,128]{3,2,1,0:T(8,128)(2,1)S(1)}, u32[]{:S(2)}, u32[]{:S(2)}) async-start(bf16[16,14,16,128]{3,2,1,0:T(8,128)(2,1)} %pack.1), calls=%async_computation.3 | async-start | bytes 1835008 | tf_op jit(solution)/shard_map/all_to_all | solution.py:218
  85.0 0.0 copy-done
  85.0 2.2 %collective-permute-start.6 = (bf16[2,512,128]{2,1,0:T(8,128)(2,1)S(1)}, bf16[2,512,128]{2,1,0:T(8,128)(2,1)S(1)}, u32[]{:S(2)}, u32[]{:S(2)}) collective-permute-start(bf16[2,512,128]{2,1,0:T(8,128)(2,1)S(1)} %copy-done), channel_id=1, source_target_pairs={{0,16},{16,0},{1,17},{17,1},{2,18},{18,2},{3,19},{19,3},{4,20},{20... | collective-permute-start | bytes 786440 | tf_op jit(solution)/shard_map/ppermute | solution.py:222
  87.2 5.1 %collective-permute-start.5 = (bf16[2,512,128]{2,1,0:T(8,128)(2,1)S(1)}, bf16[2,512,128]{2,1,0:T(8,128)(2,1)S(1)}, u32[]{:S(2)}, u32[]{:S(2)}) collective-permute-start(bf16[2,512,128]{2,1,0:T(8,128)(2,1)S(1)} %copy-done), channel_id=1, source_target_pairs={{0,32},{32,0},{1,33},{33,1},{2,34},{34,2},{3,35},{35,3},{4,36},{36... | collective-permute-start | bytes 786440 | tf_op jit(solution)/shard_map/ppermute | solution.py:223
  92.3 22.9 %collective-permute-done.6.refs_2_ = bf16[2,512,128]{2,1,0:T(8,128)(2,1)S(1)} collective-permute-done((bf16[2,512,128]{2,1,0:T(8,128)(2,1)S(1)}, bf16[2,512,128]{2,1,0:T(8,128)(2,1)S(1)}, u32[]{:S(2)}, u32[]{:S(2)}) %collective-permute-start.6) | collective-permute-done | bytes 262176 | tf_op jit(solution)/shard_map/ppermute | solution.py:222
  115.2 2.4 %collective-permute-start.7 = (bf16[2,512,128]{2,1,0:T(8,128)(2,1)S(1)}, bf16[2,512,128]{2,1,0:T(8,128)(2,1)S(1)}, u32[]{:S(2)}, u32[]{:S(2)}) collective-permute-start(bf16[2,512,128]{2,1,0:T(8,128)(2,1)S(1)} %collective-permute-done.6.refs_2_), channel_id=1, source_target_pairs={{0,32},{32,0},{1,33},{33,1},{2,34},{34,2},{3,35},{35,3},{4,36},{36... | collective-permute-start | bytes 786440 | tf_op jit(solution)/shard_map/ppermute | solution.py:224
  117.6 0.0 collective-permute-done.5.refs_1_
  117.7 1.1 collective-permute-done.7.refs_3_
  118.8 0.0 all-to-all-done.3.held
  118.8 1.2 first_contract.1
  119.9 5.0 %all-to-all-start.4 = ((bf16[32,2,16,128]{3,2,1,0:T(8,128)(2,1)}), bf16[32,2,16,128]{3,2,1,0:T(8,128)(2,1)S(1)}, u32[]{:S(2)}, u32[]{:S(2)}) async-start(bf16[32,2,16,128]{3,2,1,0:T(8,128)(2,1)} %bitcast.4), calls=%async_computation.4 | async-start | bytes 524288 | tf_op jit(solution)/shard_map/all_to_all | solution.py:218
  125.0 2.1 %collective-permute-start.4 = (bf16[16,8,16,128]{3,2,1,0:T(8,128)(2,1)S(1)}, bf16[16,8,16,128]{3,2,1,0:T(8,128)(2,1)S(1)}, u32[]{:S(2)}, u32[]{:S(2)}) collective-permute-start(bf16[16,8,16,128]{3,2,1,0:T(8,128)(2,1)S(1)} %slice.9.own), channel_id=1, source_target_pairs={{0,32},{32,0},{1,33},{33,1},{2,34},{34,2},{3,35},{35,3},{4,36},{36... | collective-permute-start | bytes 1572872 | tf_op jit(solution)/shard_map/ppermute | solution.py:236
  127.1 1.7 %collective-permute-done.4.other = bf16[16,8,16,128]{3,2,1,0:T(8,128)(2,1)S(1)} collective-permute-done((bf16[16,8,16,128]{3,2,1,0:T(8,128)(2,1)S(1)}, bf16[16,8,16,128]{3,2,1,0:T(8,128)(2,1)S(1)}, u32[]{:S(2)}, u32[]{:S(2)}) %collective-permute-start.4) | collective-permute-done | bytes 524320 | tf_op jit(solution)/shard_map/ppermute | solution.py:236
  128.8 7.0 %all-to-all-done.4.state = bf16[32,2,16,128]{3,2,1,0:T(8,128)(2,1)S(1)} async-done(((bf16[32,2,16,128]{3,2,1,0:T(8,128)(2,1)}), bf16[32,2,16,128]{3,2,1,0:T(8,128)(2,1)S(1)}, u32[]{:S(2)}, u32[]{:S(2)}) %all-to-all-start.4) | async-done | bytes 262176 | tf_op jit(solution)/shard_map/all_to_all | solution.py:218
  135.7 1.1 contract.2
  136.9 5.6 %all-to-all-start.5 = ((bf16[32,2,16,128]{3,2,1,0:T(8,128)(2,1)}), bf16[32,2,16,128]{3,2,1,0:T(8,128)(2,1)S(1)}, u32[]{:S(2)}, u32[]{:S(2)}) async-start(bf16[32,2,16,128]{3,2,1,0:T(8,128)(2,1)} %contract.2), calls=%async_computation.5 | async-start | bytes 524288 | tf_op jit(solution)/shard_map/all_to_all | solution.py:218
  142.6 4.6 %collective-permute-start.1 = (bf16[16,2,16,128]{3,2,1,0:T(8,128)(2,1)S(1)}, bf16[16,2,16,128]{3,2,1,0:T(8,128)(2,1)S(1)}, u32[]{:S(2)}, u32[]{:S(2)}) collective-permute-start(bf16[16,2,16,128]{3,2,1,0:T(8,128)(2,1)S(1)} %get-tuple-element.6), channel_id=1, source_target_pairs={{0,2},{1,3},{2,0},{3,1},{4,6},{5,7},{6,4},{7,5},{8,10},{9,11},{10,... | collective-permute-start | bytes 393224 | tf_op jit(solution)/shard_map/ppermute | solution.py:241
  147.2 2.2 %collective-permute-start = (bf16[16,2,16,128]{3,2,1,0:T(8,128)(2,1)S(1)}, bf16[16,2,16,128]{3,2,1,0:T(8,128)(2,1)S(1)}, u32[]{:S(2)}, u32[]{:S(2)}) collective-permute-start(bf16[16,2,16,128]{3,2,1,0:T(8,128)(2,1)S(1)} %get-tuple-element.6), channel_id=1, source_target_pairs={{0,1},{1,2},{2,3},{3,0},{4,5},{5,6},{6,7},{7,4},{8,9},{9,10},{10,1... | collective-permute-start | bytes 393224 | tf_op jit(solution)/shard_map/ppermute | solution.py:241
  149.4 4.3 %collective-permute-start.2 = (bf16[16,2,16,128]{3,2,1,0:T(8,128)(2,1)S(1)}, bf16[16,2,16,128]{3,2,1,0:T(8,128)(2,1)S(1)}, u32[]{:S(2)}, u32[]{:S(2)}) collective-permute-start(bf16[16,2,16,128]{3,2,1,0:T(8,128)(2,1)S(1)} %get-tuple-element.6), channel_id=1, source_target_pairs={{0,3},{1,0},{2,1},{3,2},{4,7},{5,4},{6,5},{7,6},{8,11},{9,8},{10,9... | collective-permute-start | bytes 393224 | tf_op jit(solution)/shard_map/ppermute | solution.py:241
  153.7 0.0 collective-permute-done.1
  153.7 1.0 collective-permute-done
  154.7 1.0 collective-permute-done.2
  155.7 0.1 pad_maximum_fusion.own
  155.8 4.3 %collective-permute-start.3 = (bf16[4,16,2,16,128]{4,3,2,1,0:T(8,128)(2,1)S(1)}, bf16[4,16,2,16,128]{4,3,2,1,0:T(8,128)(2,1)S(1)}, u32[]{:S(2)}, u32[]{:S(2)}) collective-permute-start(bf16[4,16,2,16,128]{4,3,2,1,0:T(8,128)(2,1)S(1)} %pad_maximum_fusion.own), channel_id=1, source_target_pairs={{0,32},{32,0},{1,33},{33,1},{2,34},{34,2},{3,35},{35,3},{4,36},{36... | collective-permute-start | bytes 1572872 | tf_op jit(solution)/shard_map/ppermute | solution.py:243
  160.1 1.5 collective-permute-done.3.other
  161.7 0.0 all-to-all-done.5.state
  161.7 1.1 contract.3
  (2 shorter events, 0.1 us)
Async XLA Ops:
  0.0 24.9 %copy-start.1 = (s32[3]{0:T(128)S(1)}, s32[3]{0:T(128)}, u32[]{:S(2)}) copy-start(s32[3]{0:T(128)} %owners.3) | copy-start | bytes 40
  2.7 82.3 %copy-start = (bf16[2,512,128]{2,1,0:T(8,128)(2,1)S(1)}, bf16[2,512,128]{2,1,0:T(8,128)(2,1)}, u32[]{:S(2)}) copy-start(bf16[2,512,128]{2,1,0:T(8,128)(2,1)} %refs_0_.1) | copy-start | bytes 786436
  80.1 38.7 %all-to-all-start.3 = ((bf16[16,14,16,128]{3,2,1,0:T(8,128)(2,1)}), bf16[16,14,16,128]{3,2,1,0:T(8,128)(2,1)S(1)}, u32[]{:S(2)}, u32[]{:S(2)}) async-start(bf16[16,14,16,128]{3,2,1,0:T(8,128)(2,1)} %pack.1), calls=%async_computation.3 | async-start | bytes 1835008 | tf_op jit(solution)/shard_map/all_to_all | solution.py:218
  85.0 30.3 %collective-permute-start.6 = (bf16[2,512,128]{2,1,0:T(8,128)(2,1)S(1)}, bf16[2,512,128]{2,1,0:T(8,128)(2,1)S(1)}, u32[]{:S(2)}, u32[]{:S(2)}) collective-permute-start(bf16[2,512,128]{2,1,0:T(8,128)(2,1)S(1)} %copy-done), channel_id=1, source_target_pairs={{0,16},{16,0},{1,17},{17,1},{2,18},{18,2},{3,19},{19,3},{4,20},{20... | collective-permute-start | bytes 786440 | tf_op jit(solution)/shard_map/ppermute | solution.py:222
  87.2 30.4 %collective-permute-start.5 = (bf16[2,512,128]{2,1,0:T(8,128)(2,1)S(1)}, bf16[2,512,128]{2,1,0:T(8,128)(2,1)S(1)}, u32[]{:S(2)}, u32[]{:S(2)}) collective-permute-start(bf16[2,512,128]{2,1,0:T(8,128)(2,1)S(1)} %copy-done), channel_id=1, source_target_pairs={{0,32},{32,0},{1,33},{33,1},{2,34},{34,2},{3,35},{35,3},{4,36},{36... | collective-permute-start | bytes 786440 | tf_op jit(solution)/shard_map/ppermute | solution.py:223
  115.2 3.5 %collective-permute-start.7 = (bf16[2,512,128]{2,1,0:T(8,128)(2,1)S(1)}, bf16[2,512,128]{2,1,0:T(8,128)(2,1)S(1)}, u32[]{:S(2)}, u32[]{:S(2)}) collective-permute-start(bf16[2,512,128]{2,1,0:T(8,128)(2,1)S(1)} %collective-permute-done.6.refs_2_), channel_id=1, source_target_pairs={{0,32},{32,0},{1,33},{33,1},{2,34},{34,2},{3,35},{35,3},{4,36},{36... | collective-permute-start | bytes 786440 | tf_op jit(solution)/shard_map/ppermute | solution.py:224
  119.9 15.8 %all-to-all-start.4 = ((bf16[32,2,16,128]{3,2,1,0:T(8,128)(2,1)}), bf16[32,2,16,128]{3,2,1,0:T(8,128)(2,1)S(1)}, u32[]{:S(2)}, u32[]{:S(2)}) async-start(bf16[32,2,16,128]{3,2,1,0:T(8,128)(2,1)} %bitcast.4), calls=%async_computation.4 | async-start | bytes 524288 | tf_op jit(solution)/shard_map/all_to_all | solution.py:218
  125.0 3.8 %collective-permute-start.4 = (bf16[16,8,16,128]{3,2,1,0:T(8,128)(2,1)S(1)}, bf16[16,8,16,128]{3,2,1,0:T(8,128)(2,1)S(1)}, u32[]{:S(2)}, u32[]{:S(2)}) collective-permute-start(bf16[16,8,16,128]{3,2,1,0:T(8,128)(2,1)S(1)} %slice.9.own), channel_id=1, source_target_pairs={{0,32},{32,0},{1,33},{33,1},{2,34},{34,2},{3,35},{35,3},{4,36},{36... | collective-permute-start | bytes 1572872 | tf_op jit(solution)/shard_map/ppermute | solution.py:236
  136.9 24.8 %all-to-all-start.5 = ((bf16[32,2,16,128]{3,2,1,0:T(8,128)(2,1)}), bf16[32,2,16,128]{3,2,1,0:T(8,128)(2,1)S(1)}, u32[]{:S(2)}, u32[]{:S(2)}) async-start(bf16[32,2,16,128]{3,2,1,0:T(8,128)(2,1)} %contract.2), calls=%async_computation.5 | async-start | bytes 524288 | tf_op jit(solution)/shard_map/all_to_all | solution.py:218
  142.6 11.2 %collective-permute-start.1 = (bf16[16,2,16,128]{3,2,1,0:T(8,128)(2,1)S(1)}, bf16[16,2,16,128]{3,2,1,0:T(8,128)(2,1)S(1)}, u32[]{:S(2)}, u32[]{:S(2)}) collective-permute-start(bf16[16,2,16,128]{3,2,1,0:T(8,128)(2,1)S(1)} %get-tuple-element.6), channel_id=1, source_target_pairs={{0,2},{1,3},{2,0},{3,1},{4,6},{5,7},{6,4},{7,5},{8,10},{9,11},{10,... | collective-permute-start | bytes 393224 | tf_op jit(solution)/shard_map/ppermute | solution.py:241
  147.2 7.5 %collective-permute-start = (bf16[16,2,16,128]{3,2,1,0:T(8,128)(2,1)S(1)}, bf16[16,2,16,128]{3,2,1,0:T(8,128)(2,1)S(1)}, u32[]{:S(2)}, u32[]{:S(2)}) collective-permute-start(bf16[16,2,16,128]{3,2,1,0:T(8,128)(2,1)S(1)} %get-tuple-element.6), channel_id=1, source_target_pairs={{0,1},{1,2},{2,3},{3,0},{4,5},{5,6},{6,7},{7,4},{8,9},{9,10},{10,1... | collective-permute-start | bytes 393224 | tf_op jit(solution)/shard_map/ppermute | solution.py:241
  149.4 6.3 %collective-permute-start.2 = (bf16[16,2,16,128]{3,2,1,0:T(8,128)(2,1)S(1)}, bf16[16,2,16,128]{3,2,1,0:T(8,128)(2,1)S(1)}, u32[]{:S(2)}, u32[]{:S(2)}) collective-permute-start(bf16[16,2,16,128]{3,2,1,0:T(8,128)(2,1)S(1)} %get-tuple-element.6), channel_id=1, source_target_pairs={{0,3},{1,0},{2,1},{3,2},{4,7},{5,4},{6,5},{7,6},{8,11},{9,8},{10,9... | collective-permute-start | bytes 393224 | tf_op jit(solution)/shard_map/ppermute | solution.py:241
  155.8 5.9 %collective-permute-start.3 = (bf16[4,16,2,16,128]{4,3,2,1,0:T(8,128)(2,1)S(1)}, bf16[4,16,2,16,128]{4,3,2,1,0:T(8,128)(2,1)S(1)}, u32[]{:S(2)}, u32[]{:S(2)}) collective-permute-start(bf16[4,16,2,16,128]{4,3,2,1,0:T(8,128)(2,1)S(1)} %pad_maximum_fusion.own), channel_id=1, source_target_pairs={{0,32},{32,0},{1,33},{33,1},{2,34},{34,2},{3,35},{35,3},{4,36},{36... | collective-permute-start | bytes 1572872 | tf_op jit(solution)/shard_map/ppermute | solution.py:243
